TPU v7x, 32 devices: a whole 2x2x4 slice. The times are simulated.
32 devices in a mesh: dp: 32 (over z, y, x, core).
Axes of the slice: x: 2, y: 2, z: 4, core: 2. Of those that a mesh axis runs over, the one named last changes fastest.
Arguments:
- tokens: bfloat16 [16384, 384], P('dp'), may hold values from -6 to 6
- gain_attn: bfloat16 [384], P('dp'), may hold values from 0.5 to 1.5
- w_qkv: bfloat16 [384, 1152], P('dp'), may hold values from -0.3125 to 0.3125
- w_proj: bfloat16 [384, 384], P('dp'), may hold values from -0.875 to 0.875
- gain_moe: bfloat16 [384], P('dp'), may hold values from 0.5 to 1.5
- w_router: bfloat16 [384, 8], P('dp'), may hold values from -0.3125 to 0.3125
- w_in: bfloat16 [32, 384, 384], P('dp'), may hold values from -0.3125 to 0.3125
- w_out: bfloat16 [32, 384, 384], P('dp'), may hold values from -1.25 to 1.25
- cotangent: bfloat16 [16384, 384], P('dp'), may hold values from -6 to 6
- image_ids: int32 [16384], P('dp'), may hold values from 0 to 109, never falling along the last dimension, each value on 1 to 197 neighbouring positions
- expert_ids: int32 [16384, 2], P('dp'), may hold values from 0 to 7, as said below
- slots: int32 [16384, 2], P('dp'), may hold values from -1 to 159, as said below
Outputs:
- mixed: bfloat16 [16384, 384], P('dp')
- grad_tokens: bfloat16 [16384, 384], P('dp')
- grad_gain_attn: float32 [384], P('dp')
- grad_w_qkv: float32 [384, 1152], P('dp')
- grad_w_proj: float32 [384, 384], P('dp')
- grad_gain_moe: float32 [384], P('dp')
- grad_w_router: float32 [384, 8], P('dp')
- grad_w_in: float32 [32, 384, 384], P('dp')
- grad_w_out: float32 [32, 384, 384], P('dp')
Inputs may be any that keep to these rules, and one draw needn't show every extreme that they name: `image_ids`: image numbers never fall along the rows; an image has 1 to 197 rows, and some image has exactly 197. `expert_ids`: the two experts of a row differ. Within one device's 512 rows, the choices naming an expert take slots 0, 1, 2, ... in the order of all first choices by row, then all second choices by row; choices beyond 160 get -1; in every draw some expert gets all 160 slots from every device.
All inputs are finite; a program needn't handle non-finite values.
Results may differ from a plain program's by a relative error of at most 0.017.
Values may be sent and summed in bfloat16 or wider, within the bound.
No kernel may reach another device: no remote copies, remote signals or barrier semaphores. Data moves between devices by JAX's collectives and lax.ppermute only.
A program may use at most 128 MiB of HBM per device.

v0:
```python
import functools

import jax
import jax.numpy as jnp
import numpy as np
from jax import lax
from jax.experimental import pallas as pl
from jax.experimental.pallas import tpu as pltpu
from jax.sharding import PartitionSpec as P

HEAD_DIM = 64
LEN = 197
EPSILON = 1e-06
MASKED = -1e30
HALO = 256
BLOCK = 128
WINDOW = BLOCK + 2 * HALO
LANES = 128
SCALE = HEAD_DIM ** (-0.5)
BF = jnp.bfloat16
F32 = jnp.float32
GELU_C = (2.0 / np.pi) ** 0.5
GELU_A = 0.044715


def dot(left, right, left_dim=1, right_dim=0):
    return lax.dot_general(
        left,
        right,
        (((left_dim,), (right_dim,)), ((), ())),
        preferred_element_type=F32,
    )


def call(body, outs, ins, scratch=(), flops=0, name=None, vmem_mib=12, fetch=False):
    vmem = pl.BlockSpec(memory_space=pltpu.VMEM)
    spec = pl.BlockSpec(memory_space=pltpu.HBM) if fetch else vmem
    if fetch:
        ins = [pltpu.with_memory_space_constraint(x, pltpu.HBM) for x in ins]
    return pl.pallas_call(
        body,
        out_shape=tuple(outs),
        in_specs=[spec] * len(ins),
        out_specs=tuple([vmem] * len(outs)),
        scratch_shapes=list(scratch),
        compiler_params=pltpu.CompilerParams(vmem_limit_bytes=vmem_mib * 1024 * 1024),
        cost_estimate=pl.CostEstimate(flops=int(flops), bytes_accessed=1024, transcendentals=0),
        name=name,
    )(*ins)


def shape(dims, dtype):
    return jax.ShapeDtypeStruct(dims, dtype)


def lane_iota(rows, lanes=LANES):
    return lax.broadcasted_iota(jnp.int32, (rows, lanes), 1)


def fetched(refs, held, sems):
    copies = [
        pltpu.make_async_copy(ref, into, sems.at[index])
        for index, (ref, into) in enumerate(zip(refs, held))
    ]
    for copy in copies:
        copy.start()
    for copy in copies:
        copy.wait()


def pack_body(experts, *refs):
    count = 7
    (out, own, low, high), held, sems = refs[count : count + 4], refs[count + 4 : -1], refs[-1]
    fetched(refs[:count], held, sems)
    w_qkv, w_proj, router_turned, gain_attn, gain_moe, tokens, ids = held
    share, cols = w_qkv.shape
    width = cols // 3
    out[:, :cols] = w_qkv[...]
    out[:, cols : 4 * width] = w_proj[...]
    lanes = lane_iota(share)
    diagonal = lax.broadcasted_iota(jnp.int32, (share, share), 0) == lane_iota(share, share)
    pick = lax.broadcasted_iota(jnp.int32, (experts, LANES), 0) == lane_iota(experts)
    tail = dot(router_turned[...], pick.astype(F32).astype(BF), 0, 0)
    for index, gain in enumerate((gain_attn, gain_moe)):
        column = jnp.sum(
            jnp.where(diagonal, gain[...].astype(F32), 0.0), axis=1, keepdims=True
        )
        tail = jnp.where(lanes == experts + index, column, tail)
    out[:, 4 * width :] = tail.astype(BF)
    rows = tokens.shape[0]
    own[:, :width] = tokens[...]
    for index in range(rows // BLOCK):
        line = (ids[index : index + 1, :] + 1).astype(F32)
        column = jnp.broadcast_to(line, (BLOCK, BLOCK)).T
        upper = jnp.floor(column * (1.0 / 256.0))
        lower = column - 256.0 * upper
        own[index * BLOCK : (index + 1) * BLOCK, width:] = jnp.where(
            lane_iota(BLOCK) == 0, upper, lower
        ).astype(BF)
    low[...] = own[rows - HALO :, :]
    high[...] = own[:HALO, :]


def quarter_body(width, w_in, w_out, quarter, sems):
    fetched(
        (w_in.at[0], w_out.at[0]), (quarter.at[:width, :], quarter.at[width:, :]), sems
    )


def join_body(parts, *refs):
    pieces, outs = refs[:-parts], refs[-parts:]
    whole = jnp.concatenate([piece[...].astype(F32) for piece in pieces], axis=0).astype(BF)
    size = whole.shape[0] // parts
    for index, out in enumerate(outs):
        out[...] = whole[index * size : (index + 1) * size, :]


def prepare_body(
    width,
    experts,
    capacity,
    own,
    low,
    high,
    order,
    experts_row,
    slots_row,
    xhat,
    rstd_out,
    select,
    idcol,
    idrow,
    routes,
    place_row,
):
    me = lax.axis_index("dp")
    devices = 4 * experts
    share = width // devices
    target = (me ^ order[0:1, :]) * share + order[1:2, :]
    sel = (lax.broadcasted_iota(jnp.int32, (width, width), 0) == target).astype(F32).astype(BF)
    select[...] = sel
    start = 0
    for ref in (low, own, high):
        rows = ref.shape[0]
        values = dot(ref[:, :width], sel)
        mean = jnp.mean(values, axis=1, keepdims=True)
        centered = values - mean
        rstd = lax.rsqrt(jnp.mean(centered * centered, axis=1, keepdims=True) + EPSILON)
        xhat[start : start + rows, :] = centered * rstd
        rstd_out[start : start + rows, :] = jnp.broadcast_to(rstd, (rows, LANES))
        marks = ref[:, width : width + LANES].astype(F32)
        column = marks[:, 0:1] * 256.0 + marks[:, 1:2]
        idcol[start : start + rows, :] = jnp.broadcast_to(column, (rows, LANES))
        turned = marks.T
        line = turned[0:1, :] * 256.0 + turned[1:2, :]
        idrow[:, start : start + rows] = jnp.broadcast_to(line, (8, rows))
        start += rows
    rows = own.shape[0]
    group = (((me >> 2) & (experts // 2 - 1)) << 1) | (me & 1)
    half_bits = (experts // 2).bit_length() - 1
    expert = experts_row[...]
    slot = slots_row[...]
    holder = ((expert & (experts // 2 - 1)) << 1) | (expert >> half_bits)
    apart = group ^ holder
    index = (apart & 1) * (experts // 2) + (apart >> 1)
    place = jnp.where(slot >= 0, index * capacity + slot, -1).astype(F32)
    lines = jnp.concatenate(
        [place, expert.astype(F32), jnp.zeros((4, rows), F32)], axis=0
    )
    place_row[...] = lines
    routes[...] = jnp.concatenate([lines] * (LANES // 8), axis=0).T


def stacked(values, half):
    zero = jnp.zeros_like(values)
    return jnp.concatenate(
        [jnp.where(half, values, zero), jnp.where(half, zero, values)], axis=0
    )


def forward_body(
    width,
    experts,
    capacity,
    xhat,
    idcol,
    idrow,
    select,
    own,
    cotangent,
    routes,
    place_row,
    near_one,
    near_two,
    far_one,
    far_two,
    *outs,
):
    same_core, other_core, outs = outs[0], outs[1 : 1 + experts // 2], outs[1 + experts // 2 :]
    qkv, attended, lse, middle, normed_two, probs, normed, weights, weights_tail, gain = outs
    rows = own.shape[0]
    span = xhat.shape[0]
    cols = 3 * width
    parts = (near_one, near_two, far_one, far_two)
    size = width // 4
    for index, part in enumerate(parts):
        weights[index * size : (index + 1) * size, :] = part[:, :cols]
    sel = select[...]
    tail = jnp.concatenate([part[:, cols:] for part in parts], axis=0)
    gain_row = tail[:, width:].astype(F32).T[experts : experts + 1, :]
    gain[...] = jnp.broadcast_to(gain_row, (8, width))
    natural = dot(sel, tail)
    weights_tail[...] = natural.astype(BF)
    gain_two = natural[:, width:].T[experts + 1 : experts + 2, :]
    normed[...] = (xhat[...] * gain_row).astype(BF)
    qkv[HALO : HALO + rows, :] = dot(normed[HALO : HALO + rows, :], weights[...]).astype(BF)
    for first in (0, HALO + rows):
        qkv[first : first + HALO, width:] = dot(
            normed[first : first + HALO, :], weights[:, width:]
        ).astype(BF)
    half = lane_iota(BLOCK) < HEAD_DIM

    def attend(block, carry):
        base = pl.multiple_of(block * BLOCK, BLOCK)
        window = pl.ds(base, WINDOW)
        here = pl.ds(base, BLOCK)
        marks = idrow[0:1, pl.ds(base + HALO, BLOCK)]
        same = idcol[window, 0:1] == jnp.concatenate([marks, marks], axis=1)
        for pair in range(width // LANES):
            start = pair * LANES
            queries = qkv[pl.ds(base + HALO, BLOCK), start : start + LANES]
            queries = stacked((queries.astype(F32) * SCALE).astype(BF), half)
            keys = qkv[window, width + start : width + start + LANES]
            values = qkv[window, 2 * width + start : 2 * width + start + LANES]
            scores = jnp.where(same, dot(keys, queries, 1, 1), MASKED)
            peak = jnp.max(scores, axis=0, keepdims=True)
            raised = jnp.exp(scores - peak)
            total = jnp.sum(raised, axis=0, keepdims=True)
            result = dot(raised.astype(BF), values, 0, 0)
            column = jnp.broadcast_to(1.0 / total, (8, 2 * BLOCK)).T[:, 0:1]
            result = result * column
            attended[here, start : start + LANES] = jnp.where(
                half, result[:BLOCK], result[BLOCK:]
            ).astype(BF)
            logs = peak + jnp.log(total)
            lse[2 * pair : 2 * pair + 1, here] = logs[:, :BLOCK]
            lse[2 * pair + 1 : 2 * pair + 2, here] = logs[:, BLOCK:]
        return carry

    lax.fori_loop(0, rows // BLOCK, attend, 0, unroll=4)
    mid = own[:, :width].astype(F32) + dot(attended[...], weights_tail[:, :width])
    middle[...] = mid
    centered = mid - jnp.mean(mid, axis=1, keepdims=True)
    variance = jnp.mean(centered * centered, axis=1, keepdims=True)
    low_two = (centered * lax.rsqrt(variance + EPSILON) * gain_two).astype(BF)
    normed_two[...] = low_two
    lanes = lane_iota(rows)
    logits = jnp.where(lanes < experts, dot(low_two, weights_tail[:, width:]), MASKED)
    raised = jnp.exp(logits - jnp.max(logits, axis=1, keepdims=True))
    share = raised / jnp.sum(raised, axis=1, keepdims=True)
    probs[...] = share
    upstream = cotangent[...].astype(F32)
    wide_lanes = lanes.astype(F32)
    gates = []
    for choice in range(2):
        gate = jnp.sum(
            jnp.where(wide_lanes == routes[:, 2 + choice : 3 + choice], share, 0.0),
            axis=1,
            keepdims=True,
        )
        gates.append(jnp.broadcast_to(gate, (rows, 8)))
    gates = jnp.concatenate(gates + [jnp.zeros((rows, LANES - 16), F32)], axis=1).T
    source = jnp.concatenate([low_two, cotangent[...]], axis=1)
    for index in range(experts):
        if index < experts // 2:
            chunk = same_core.at[index * capacity : (index + 1) * capacity, :]
        else:
            chunk = other_core[index - experts // 2]
        slot = (
            lax.broadcasted_iota(jnp.int32, (capacity, rows), 0) + index * capacity
        ).astype(F32)
        first = slot == place_row[0:1, :]
        second = slot == place_row[1:2, :]
        weight = jnp.where(first, gates[0:1, :], jnp.where(second, gates[8:9, :], 0.0))
        taken = jnp.where(first | second, 1.0, 0.0)
        moved = dot(taken.astype(BF), source)
        chunk[:, :width] = moved[:, :width].astype(BF)
        chunk[:, width:] = (
            moved[:, width:] * jnp.sum(weight, axis=1, keepdims=True)
        ).astype(BF)


def joined(pieces, held):
    capacity = pieces[0].shape[0]
    for index, piece in enumerate(pieces):
        held[index * capacity : (index + 1) * capacity, :] = piece[...]


def expert_body(width, tile, count, *refs):
    pieces, kept, sent, rest = (
        refs[:count],
        refs[count],
        refs[count + 1 : count + 5],
        refs[count + 5 :],
    )
    returns, (hidden_out, grad_out, arrived, back, w_in, w_out) = rest[:count], rest[count:]
    joined(pieces, arrived)
    w_ins = [kept.at[:width, :], kept.at[2 * width : 3 * width, :], sent[0], sent[2]]
    w_outs = [kept.at[width : 2 * width, :], kept.at[3 * width :, :], sent[1], sent[3]]
    for quarter, (first, second) in enumerate(zip(w_ins, w_outs)):
        at = slice(quarter * width, (quarter + 1) * width)
        w_in[:, at] = first[...]
        w_out[at, :] = second[...]
    step_width = 2 * width // 3

    def step(index, carry):
        at = pl.ds(pl.multiple_of(index * tile, tile), tile)
        for start in range(0, 4 * width, step_width):
            columns = slice(start, start + step_width)
            pre = dot(arrived[at, :width], w_in[:, columns])
            hidden_grad = dot(arrived[at, width:], w_out[columns, :], 1, 1)
            square = pre * pre
            bend = jnp.tanh(pre * (GELU_C + (GELU_C * GELU_A) * square))
            scaled = 0.5 * pre
            hidden_out[at, columns] = (scaled + scaled * bend).astype(BF)
            slope = (0.5 + 0.5 * bend) + (
                scaled * (GELU_C + (3.0 * GELU_C * GELU_A) * square)
            ) * (1.0 - bend * bend)
            grad_out[at, columns] = (hidden_grad * slope).astype(BF)
        back[at, :width] = dot(hidden_out[at, :], w_out[...]).astype(BF)
        back[at, width:] = dot(grad_out[at, :], w_in[...], 1, 1).astype(BF)
        return carry

    lax.fori_loop(0, arrived.shape[0] // tile, step, 0)
    capacity = pieces[0].shape[0]
    for index, out in enumerate(returns):
        out[...] = back[index * capacity : (index + 1) * capacity, :]


def expert_grad_body(width, count, *refs):
    pieces, (hidden_one, hidden_two, pre_one, pre_two, kept, sent) = refs[:count], refs[count:]
    size = 2 * width
    outs = (kept.at[:size, :], kept.at[size:, :], sent.at[:size, :], sent.at[size:, :])
    grad_in = grad_out = 0.0
    for part, hidden, pre_grad in (
        (pieces[: count // 2], hidden_one, pre_one),
        (pieces[count // 2 :], hidden_two, pre_two),
    ):
        rows = jnp.concatenate([piece[:, :width] for piece in part], axis=0)
        grads = jnp.concatenate([piece[:, width:] for piece in part], axis=0)
        grad_in = grad_in + dot(rows, pre_grad[...], 0, 0)
        grad_out = grad_out + dot(grads, hidden[...], 0, 0)
    for quarter, out in enumerate(outs):
        columns = slice(quarter * width, (quarter + 1) * width)
        out[:width, :] = grad_in[:, columns].astype(BF)
        out[width:, :] = grad_out[:, columns].T.astype(BF)


def at_home(half):
    me = lax.axis_index("dp")
    return (me >= half) == ((me & 1) == 1)


def halve_body(whole, upper, lower):
    size = upper.shape[0]
    upper[...] = whole[:size, :]
    lower[...] = whole[size:, :]


def choose_body(half, size, near_one, near_in, near_out, *refs):
    far, kept, sent = refs[:4], refs[4], refs[5:]
    near = (near_one.at[:size, :], near_one.at[size:, :], near_in, near_out)

    def place(mine, theirs):
        for index, (one, two) in enumerate(zip(mine, theirs)):
            kept[index * size : (index + 1) * size, :] = one[...]
            sent[index][...] = two[...]

    @pl.when(at_home(half))
    def _():
        place(near, far)

    @pl.when(jnp.logical_not(at_home(half)))
    def _():
        place(far, near)


def mix_body(capacity, mine, *refs):
    theirs, outs = refs[: len(refs) // 2], refs[len(refs) // 2 :]
    for index, (part, out) in enumerate(zip(theirs, outs)):
        out[:capacity, :] = mine[index * capacity : (index + 1) * capacity, :]
        out[capacity:, :] = part[...]


def unmix_body(capacity, *refs):
    count = len(refs) // 2
    pieces, mine, theirs = refs[:count], refs[count], refs[count + 1 :]
    for index, (piece, out) in enumerate(zip(pieces, theirs)):
        mine[index * capacity : (index + 1) * capacity, :] = piece[:capacity, :]
        out[...] = piece[capacity:, :]


def split_body(half, size, mine, theirs, weights, normed, *outs):
    home_one, home_two, home_three, *away, keys_turned = outs
    width = size // 2
    keys_turned[...] = dot(weights[:, width : 2 * width], normed[...], 0, 1).astype(BF)

    def place(home, other):
        home_one[...] = home[:size, :]
        home_two[...], home_three[...] = home[size : 3 * size // 2, :], home[3 * size // 2 :, :]
        away[0][...] = other[:size, :]
        away[1][...], away[2][...] = other[size : 3 * size // 2, :], other[3 * size // 2 :, :]

    @pl.when(at_home(half))
    def _():
        place(mine, theirs)

    @pl.when(jnp.logical_not(at_home(half)))
    def _():
        place(theirs, mine)


def combine_body(
    width,
    experts,
    capacity,
    middle,
    normed_two,
    probs,
    cotangent,
    routes,
    attended,
    weights_tail,
    select,
    *refs,
):
    mixed, middle_grad, attended_grad, tail_grad, held = refs[-5:]
    start = 0
    for ref in refs[:-5]:
        held[start : start + ref.shape[0], :] = ref[...]
        start += ref.shape[0]
    rows = middle.shape[0]
    slots = experts * capacity
    gain_two = weights_tail[:, width:].astype(F32).T[experts + 1 : experts + 2, :]
    gain_grad = jnp.zeros((1, width), F32)
    router_rows = []
    branch_rows = []
    tile = rows
    for start in range(0, rows, tile):
        at = slice(start, start + tile)
        lanes = lane_iota(tile).astype(F32)
        wide = lax.broadcasted_iota(jnp.int32, (tile, slots), 1).astype(F32)
        first = (wide == routes[at, 0:1]).astype(F32)
        second = (wide == routes[at, 1:2]).astype(F32)
        picked = dot(
            jnp.concatenate([first, second], axis=0).astype(BF), held[:, :width]
        )
        grad_two = dot((first + second).astype(BF), held[:, width:])
        upstream = cotangent[at, :].astype(F32)
        share = probs[at, :]
        mid = middle[at, :]
        total = mid
        probs_grad = jnp.zeros((tile, LANES), F32)
        for choice in range(2):
            chosen = lanes == routes[at, 2 + choice : 3 + choice]
            gate = jnp.sum(jnp.where(chosen, share, 0.0), axis=1, keepdims=True)
            one = picked[choice * tile : (choice + 1) * tile, :]
            total = total + gate * one
            gate_grad = jnp.sum(one * upstream, axis=1, keepdims=True)
            probs_grad = probs_grad + jnp.where(chosen, gate_grad, 0.0)
        mixed[at, :] = total.astype(BF)
        logits_grad = (
            share * (probs_grad - jnp.sum(share * probs_grad, axis=1, keepdims=True))
        ).astype(BF)
        router_rows.append(logits_grad)
        grad_two = grad_two + dot(logits_grad, weights_tail[:, width:], 1, 1)
        centered = mid - jnp.mean(mid, axis=1, keepdims=True)
        variance = jnp.mean(centered * centered, axis=1, keepdims=True)
        rstd = lax.rsqrt(variance + EPSILON)
        xhat = centered * rstd
        gain_grad = gain_grad + jnp.sum(grad_two * xhat, axis=0, keepdims=True)
        inner = grad_two * gain_two
        inner_grad = rstd * (
            inner
            - jnp.mean(inner, axis=1, keepdims=True)
            - xhat * jnp.mean(inner * xhat, axis=1, keepdims=True)
        )
        through = upstream + inner_grad
        middle_grad[at, :] = through
        branch = through.astype(BF)
        branch_rows.append(branch)
        attended_grad[at, :] = dot(branch, weights_tail[:, :width], 1, 1).astype(BF)
    sel = select[...]
    logits_grad = jnp.concatenate(router_rows, axis=0)
    branch = jnp.concatenate(branch_rows, axis=0)
    attended_turned = dot(attended[...], sel).astype(BF)
    normed_turned = dot(normed_two[...], sel).astype(BF)
    tail_grad[:, :width] = dot(attended_turned, branch, 0, 0).astype(BF)
    gain_line = jnp.broadcast_to(gain_grad, (8, width))
    upper = gain_line.astype(BF)
    lower = (gain_line - upper.astype(F32)).astype(BF)
    gain_turned = dot(upper, sel) + dot(lower, sel)
    gain_column = jnp.broadcast_to(gain_turned[0:1, :], (LANES, width)).T
    router_grad = dot(normed_turned, logits_grad, 0, 0)
    tail_grad[:, width:] = jnp.where(
        lane_iota(width) == experts + 1, gain_column, router_grad
    ).astype(BF)


def backward_body(
    width,
    qkv,
    keys_turned,
    lse,
    attended_grad,
    idcol,
    idrow,
    normed,
    tail_grad,
    dq,
    rims_low,
    rims_high,
    inner,
    kept,
    *sents,
):
    rows = attended_grad.shape[0]
    half_rows = width // 2
    *sents, acc = sents
    half = lane_iota(BLOCK) < HEAD_DIM
    upper = lax.broadcasted_iota(jnp.int32, (LANES, BLOCK), 0) < HEAD_DIM
    acc[...] = jnp.zeros_like(acc)

    def attend(block, carry):
        base = pl.multiple_of(block * BLOCK, BLOCK)
        window = pl.ds(base, WINDOW)
        here = pl.ds(base, BLOCK)
        marks = idrow[0:1, pl.ds(base + HALO, BLOCK)]
        same = idcol[window, 0:1] == jnp.concatenate([marks, marks], axis=1)
        for pair in range(width // LANES):
            start = pair * LANES
            queries = qkv[pl.ds(base + HALO, BLOCK), start : start + LANES]
            queries = stacked((queries.astype(F32) * SCALE).astype(BF), half)
            grads = stacked(attended_grad[here, start : start + LANES], half)
            keys = qkv[window, width + start : width + start + LANES]
            values = qkv[window, 2 * width + start : 2 * width + start + LANES]
            logs = jnp.concatenate(
                [lse[2 * pair : 2 * pair + 1, here], lse[2 * pair + 1 : 2 * pair + 2, here]], axis=1
            )
            scores = jnp.where(same, dot(keys, queries, 1, 1), MASKED)
            weights = jnp.exp(scores - logs)
            weights_grad = dot(values, grads, 1, 1)
            delta = jnp.sum(weights * weights_grad, axis=0, keepdims=True)
            scores_grad = (weights * (weights_grad - delta)).astype(BF)
            acc[window, start : start + LANES] += dot(scores_grad, queries)
            acc[window, width + start : width + start + LANES] += dot(weights.astype(BF), grads)
            result = dot(keys_turned[start : start + LANES, window], scores_grad) * SCALE
            dq[here, start : start + LANES] = (
                jnp.where(upper, result[:, :BLOCK], result[:, BLOCK:]).T.astype(BF)
            )
        return carry

    lax.fori_loop(0, rows // BLOCK, attend, 0, unroll=2)
    rims_low[...] = acc[:HALO, :].astype(BF)
    rims_high[...] = acc[HALO + rows :, :].astype(BF)
    inner[...] = acc[HALO : HALO + rows, :]
    own = normed[HALO : HALO + rows, :]
    query_part = dot(own, dq[...], 0, 0)
    kept[:, :width] = query_part[:half_rows]
    other_part = dot(normed[...], acc[...].astype(BF), 0, 0)
    kept[:, width : 3 * width] = other_part[:half_rows]
    kept[:, 3 * width :] = tail_grad[:half_rows, :].astype(F32)
    size = half_rows // len(sents)
    for index, sent in enumerate(sents):
        at = slice(half_rows + index * size, half_rows + (index + 1) * size)
        sent[:, :width] = query_part[at].astype(BF)
        sent[:, width : 3 * width] = other_part[at].astype(BF)
        sent[:, 3 * width :] = tail_grad[at, :]


def finish_body(
    width, dq, inner, from_low, from_high, weights, normed_gain, xhat, rstd, select, middle_grad, out, grad
):
    rows = dq.shape[0]
    experts_lane = 0
    grad[...] = inner[...]
    grad[:HALO, :] += from_low[...].astype(F32)
    grad[rows - HALO :, :] += from_high[...].astype(F32)
    values = dot(dq[...], weights[:, :width], 1, 1) + dot(
        grad[...].astype(BF), weights[:, width:], 1, 1
    )
    hat = xhat[HALO : HALO + rows, :]
    values = values * normed_gain[0:1, :]
    part = rstd[HALO : HALO + rows, 0:1] * (
        values
        - jnp.mean(values, axis=1, keepdims=True)
        - hat * jnp.mean(values * hat, axis=1, keepdims=True)
    )
    upper = part.astype(BF)
    lower = (part - upper.astype(F32)).astype(BF)
    sel = select[...]
    out[...] = (middle_grad[...] + dot(upper, sel, 1, 1) + dot(lower, sel, 1, 1)).astype(BF)


def sum_body(parts, own, *refs):
    arrived, outs = refs[: len(refs) - parts], refs[len(refs) - parts :]
    total = own[...].astype(F32)
    if arrived[0].shape[0] < total.shape[0]:
        total = total + jnp.concatenate([ref[...].astype(F32) for ref in arrived], axis=0)
    else:
        for ref in arrived:
            total = total + ref[...].astype(F32)
    size = total.shape[0] // parts
    for index, out in enumerate(outs):
        out[...] = total[index * size : (index + 1) * size, :].astype(out.dtype)


def final_body(width, experts, own, *refs):
    arrived, rest = refs[:-13], refs[-13:]
    w_qkv, gain, *parts, qkv_grad, proj_grad, router_grad, one, two, in_grad, out_grad = rest
    total = own[...]
    for ref in arrived:
        total = total + ref[...].astype(F32)
    qkv = total[:, : 3 * width]
    qkv_grad[...] = qkv
    proj_grad[...] = total[:, 3 * width : 4 * width]
    gain_grad = jnp.sum(qkv * w_qkv[...].astype(F32), axis=1, keepdims=True)
    tail = total[:, 4 * width :]
    share = own.shape[0]
    diagonal = lax.broadcasted_iota(jnp.int32, (share, share), 0) == lane_iota(share, share)

    def turned(column):
        return jnp.sum(jnp.where(diagonal, column, 0.0), axis=0, keepdims=True)

    one[...] = turned(gain_grad) / gain[...].astype(F32)
    two[...] = turned(tail[:, experts + 1 : experts + 2])
    for index in range(experts):
        router_grad[index : index + 1, :] = turned(tail[:, index : index + 1])
    mine, upper, lower, other = parts
    for out, at, beside in (
        (in_grad, slice(0, width), upper),
        (out_grad, slice(width, 2 * width), lower),
    ):
        out[0] = mine[at, :].astype(F32) + beside[...].astype(F32) + other[at, :].astype(F32)


def gather_stages(devices):
    bits = devices.bit_length() - 1
    stages = []
    top = bits - 1
    while top >= 1:
        if top >= 2:
            low, high = 1 << (top - 1), 1 << top
            stages.append([low, high, low | high])
            top -= 2
        else:
            stages.append([1 << top])
            top -= 1
    stages.append([1])
    return stages


def swap(value, devices, mask):
    return lax.ppermute(value, "dp", [(i, i ^ mask) for i in range(devices)])


def reduce_scattered(kept, sent, devices, stages, before, after):
    total = kept
    arrived = [swap(part, devices, stages[-1][0]) for part in sent]
    for level in range(len(stages) - 1, 0, -1):
        masks = stages[level - 1]
        parts = 1 + len(masks)
        dims = (total.shape[0] // parts, total.shape[1])
        outs = [shape(dims, F32)] + [shape(dims, BF)] * (parts - 1)
        if level == 1:
            arrived, before[-1], after = lax.optimization_barrier((arrived, before[-1], after))
        if level == 2:
            arrived, before[:-1] = lax.optimization_barrier((arrived, before[:-1]))
        pieces = call(
            functools.partial(sum_body, parts), outs, [total] + arrived, name=f"sum{level}"
        )
        total = pieces[0]
        arrived = [swap(piece, devices, mask) for piece, mask in zip(pieces[1:], masks)]
    return total, arrived, before, after


def per_device(
    tokens,
    gain_attn,
    w_qkv,
    w_proj,
    gain_moe,
    w_router,
    w_in,
    w_out,
    cotangent,
    image_ids,
    expert_ids,
    slots,
):
    devices = lax.axis_size("dp")
    experts = devices // 4
    rows, width = tokens.shape
    capacity = max(2, 5 * rows // (2 * experts))
    share = width // devices
    span = rows + 2 * HALO
    stages = gather_stages(devices)
    everyone = range(devices)
    half = devices // 2

    ins = [
        w_qkv,
        w_proj,
        w_router.T,
        gain_attn[None, :],
        gain_moe[None, :],
        tokens,
        image_ids.reshape(rows // BLOCK, BLOCK),
    ]
    packed, own, low, high = call(
        functools.partial(pack_body, experts),
        [
            shape((share, 4 * width + LANES), BF),
            shape((rows, width + LANES), BF),
            shape((HALO, width + LANES), BF),
            shape((HALO, width + LANES), BF),
        ],
        ins,
        scratch=[pltpu.VMEM(x.shape, x.dtype) for x in ins]
        + [pltpu.SemaphoreType.DMA((len(ins),))],
        name="pack",
        fetch=True,
    )
    up = [(i, i + 1) for i in range(devices - 1)]
    down = [(i + 1, i) for i in range(devices - 1)]
    low = lax.ppermute(low, "dp", up)
    high = lax.ppermute(high, "dp", down)
    packed, w_in = lax.optimization_barrier((packed, w_in))
    quarter = call(
        functools.partial(quarter_body, width),
        [shape((2 * width, width), BF)],
        [w_in, w_out],
        scratch=[pltpu.SemaphoreType.DMA((2,))],
        name="quarter",
        fetch=True,
    )[0]
    order = [0]
    near = [packed]
    far = None
    for stage in stages:
        order = [a ^ mask for mask in [0] + stage for a in order]
        arrived = [swap(part, devices, mask) for mask in stage for part in near]
        if stage is stages[0]:
            arrived[0], low, high, quarter = lax.optimization_barrier(
                (arrived[0], low, high, quarter)
            )
            arrived[1], quarter_far = lax.optimization_barrier((arrived[1], quarter))
        if stage is stages[-2]:
            *arrived, late_in = lax.optimization_barrier((*arrived, w_in[0]))
        if stage is stages[-1]:
            far = arrived
        else:
            parts = 2 if stage is stages[-2] else 1
            size = near[0].shape[0] * (1 + len(stage)) // parts
            near = call(
                functools.partial(join_body, parts),
                [shape((size, near[0].shape[1]), BF)] * parts,
                [*near, *arrived],
                name="join",
            )
    order = np.stack(
        [
            np.repeat(np.array(order, np.int32), share),
            np.tile(np.arange(share, dtype=np.int32), devices),
        ]
    )

    far_quarter = swap(quarter_far, devices, half)
    near_in = swap(late_in, devices, 2)

    def exchange(parts):
        return [parts[0]] + [
            swap(part, devices, 4 * index) for index, part in enumerate(parts) if index
        ]

    xhat, rstd, select, idcol, idrow, routes, place_row = call(
        functools.partial(prepare_body, width, experts, capacity),
        [
            shape((span, width), F32),
            shape((span, LANES), F32),
            shape((width, width), BF),
            shape((span, LANES), F32),
            shape((8, span), F32),
            shape((rows, LANES), F32),
            shape((8, rows), F32),
        ],
        [own, low, high, jnp.asarray(order), expert_ids.T, slots.T],
        flops=2 * span * width * width,
        name="prepare",
    )
    chips = experts // 2
    half_slots = chips * capacity
    outs = call(
        functools.partial(forward_body, width, experts, capacity),
        [shape((half_slots, 2 * width), BF)]
        + [shape((capacity, 2 * width), BF)] * chips
        + [
            shape((span, 3 * width), BF),
            shape((rows, width), BF),
            shape((8, rows), F32),
            shape((rows, width), F32),
            shape((rows, width), BF),
            shape((rows, LANES), F32),
            shape((span, width), BF),
            shape((width, 3 * width), BF),
            shape((width, width + LANES), BF),
            shape((8, width), F32),
        ],
        [xhat, idcol, idrow, select, own, cotangent, routes, place_row, *near, *far],
        name="forward",
    )
    same_core, other_core, outs = outs[0], outs[1 : 1 + chips], outs[1 + chips :]
    qkv, attended, lse, middle, normed_two, probs, normed, weights, weights_tail, gain = outs

    both = shape((2 * capacity, 2 * width), BF)
    *other_core, near_in = lax.optimization_barrier((*other_core, near_in))
    pieces = call(
        functools.partial(mix_body, capacity),
        [both] * chips,
        [same_core, *[swap(part, devices, 1) for part in other_core]],
        name="mix",
    )
    far_quarter, late_out, piece = lax.optimization_barrier((far_quarter, w_out[0], pieces[0]))
    near_out = swap(late_out, devices, 2)
    arrived = exchange([piece, *pieces[1:]])
    far_half = call(
        halve_body, [shape((width, width), BF)] * 2, [far_quarter], name="halve"
    )
    far_half = [*far_half] + [swap(part, devices, 2) for part in far_half]
    slot_count = experts * capacity
    pair = shape((4 * width, width), BF)
    far_half[-1], *arrived[1:-1] = lax.optimization_barrier((far_half[-1], *arrived[1:-1]))
    kept_pair, *sent_parts = call(
        functools.partial(choose_body, half, width),
        [pair] + [shape((width, width), BF)] * 4,
        [quarter, near_in, near_out, *far_half],
        name="choose",
    )
    expert_weights = [kept_pair] + [swap(part, devices, 1) for part in sent_parts]
    tile = slot_count // 4
    held = pltpu.VMEM((slot_count, 2 * width), BF)
    back, hidden, pre_grad = [], [], []
    for part in (arrived[: chips // 2], arrived[chips // 2 :]):
        half_held = pltpu.VMEM((half_slots, 2 * width), BF)
        outs = call(
            functools.partial(expert_body, width, tile, len(part)),
            [both] * len(part) + [shape((half_slots, 4 * width), BF)] * 2,
            [*part, *expert_weights],
            scratch=[
                half_held,
                half_held,
                pltpu.VMEM((width, 4 * width), BF),
                pltpu.VMEM((4 * width, width), BF),
            ],
            flops=4 * slot_count * width * 4 * width,
            name="expert",
            vmem_mib=16,
        )
        back += outs[: len(part)]
        hidden.append(outs[-2])
        pre_grad.append(outs[-1])
    returned = exchange(back)
    kept_pair, sent_pair = call(
        functools.partial(expert_grad_body, width, chips),
        [pair, pair],
        [*arrived, *hidden, *pre_grad],
        vmem_mib=16,
        flops=4 * slot_count * width * 4 * width,
        name="expert_grad",
    )
    other_pair = swap(sent_pair, devices, 1)
    single = shape((2 * width, width), BF)
    square = shape((width, width), BF)
    home_kept, *home_sent = call(
        functools.partial(split_body, half, 2 * width),
        [single, square, square] * 2 + [shape((width, span), BF)],
        [kept_pair, other_pair, weights, normed],
        name="split",
    )
    home_sent, (away_kept, *away_sent, keys_turned) = home_sent[:2], home_sent[2:]
    away_came = [swap(part, devices, 2) for part in away_sent]
    *home_sent, returned[1] = lax.optimization_barrier((*home_sent, returned[1]))
    home_came = [swap(part, devices, 2) for part in home_sent]
    away = call(
        functools.partial(sum_body, 1), [single], [away_kept, *away_came], name="away"
    )[0]

    returned[-1], away = lax.optimization_barrier((returned[-1], away))
    mine, *theirs = call(
        functools.partial(unmix_body, capacity),
        [shape((half_slots, 2 * width), BF)] + [shape((capacity, 2 * width), BF)] * chips,
        returned,
        name="unmix",
    )
    theirs = [swap(part, devices, 1) for part in theirs]
    mixed, middle_grad, attended_grad, tail_grad = call(
        functools.partial(combine_body, width, experts, capacity),
        [
            shape((rows, width), BF),
            shape((rows, width), F32),
            shape((rows, width), BF),
            shape((width, width + LANES), BF),
        ],
        [
            middle,
            normed_two,
            probs,
            cotangent,
            routes,
            attended,
            weights_tail,
            select,
            mine,
            *theirs,
        ],
        scratch=[pltpu.VMEM((slot_count, 2 * width), BF)],
        flops=6 * rows * slot_count * width,
        name="combine",
    )
    expert_parts = [home_kept, *home_came, swap(away, devices, half)]
    half_rows = width // 2

    dq, rims_low, rims_high, inner, kept, *sent = call(
        functools.partial(backward_body, width),
        [
            shape((rows, width), BF),
            shape((HALO, 2 * width), BF),
            shape((HALO, 2 * width), BF),
            shape((rows, 2 * width), F32),
            shape((half_rows, 4 * width + LANES), F32),
        ]
        + [shape((half_rows // 4, 4 * width + LANES), BF)] * 4,
        [qkv, keys_turned, lse, attended_grad, idcol, idrow, normed, tail_grad],
        scratch=[pltpu.VMEM((span, 2 * width), F32)],
        name="backward",
    )
    total, last, expert_parts, (rims_low, rims_high) = reduce_scattered(
        kept, sent, devices, stages, expert_parts, [rims_low, rims_high]
    )
    from_high = lax.ppermute(rims_low, "dp", down)
    from_low = lax.ppermute(rims_high, "dp", up)
    grad_tokens = call(
        functools.partial(finish_body, width),
        [shape((rows, width), BF)],
        [dq, inner, from_low, from_high, weights, gain, xhat, rstd, select, middle_grad],
        scratch=[pltpu.VMEM((rows, 2 * width), F32)],
        flops=2 * rows * width * 5 * width,
        name="finish",
    )[0]

    last[0], grad_tokens = lax.optimization_barrier((last[0], grad_tokens))
    qkv_grad, proj_grad, router_grad, gain_one_grad, gain_two_grad, in_grad, out_grad = call(
        functools.partial(final_body, width, experts),
        [
            shape((share, 3 * width), F32),
            shape((share, width), F32),
            shape((experts, share), F32),
            shape((1, share), F32),
            shape((1, share), F32),
            shape((1, width, width), F32),
            shape((1, width, width), F32),
        ],
        [total, *last, w_qkv, gain_attn[None, :], *expert_parts],
        name="final",
    )
    return (
        mixed,
        grad_tokens,
        gain_one_grad.reshape(share),
        qkv_grad,
        proj_grad,
        gain_two_grad.reshape(share),
        router_grad.T,
        in_grad,
        out_grad,
    )


def solution(mesh):
    row, line, cube = P("dp", None), P("dp"), P("dp", None, None)
    return jax.shard_map(
        per_device,
        mesh=mesh,
        in_specs=(row, line, row, row, line, row, cube, cube, row, line, row, row),
        out_specs=(row, row, line, row, row, line, row, cube, cube),
        check_vma=False,
    )
```

profile of v0, /device:TPU:0, one launch (start us, length us, event | category | flops | bytes accessed | tf_op | source)
XLA Modules:
  0.0 165.2 jit_solution(4216415160775087088)
XLA Ops:
  0.7 1.4 pack.1
  2.1 2.4 %collective-permute-start.1 = (bf16[256,512]{1,0:T(8,128)(2,1)S(1)}, bf16[256,512]{1,0:T(8,128)(2,1)S(1)}, u32[]{:S(2)}, u32[]{:S(2)}) collective-permute-start(bf16[256,512]{1,0:T(8,128)(2,1)S(1)} %get-tuple-element.144), channel_id=1, source_target_pairs={{0,1},{1,2},{2,3},{3,4},{4,5},{5,6},{6,7},{7,8},{8,9},{9,10},{10,1... | collective-permute-start | bytes 786440 | tf_op jit(solution)/shard_map/ppermute | solution.py:736
  4.5 1.3 collective-permute-start.2
  5.8 6.8 %collective-permute-start = (bf16[12,1664]{1,0:T(8,128)(2,1)S(1)}, bf16[12,1664]{1,0:T(8,128)(2,1)S(1)}, u32[]{:S(2)}, u32[]{:S(2)}) collective-permute-start(bf16[12,1664]{1,0:T(8,128)(2,1)S(1)} %get-tuple-element.143.refs_0_), channel_id=1, source_target_pairs={{0,8},{1,9},{2,10},{3,11},{4,12},{5,13},{6,14},{7,15},{8,0},{9,1},... | collective-permute-start | bytes 119816 | tf_op jit(solution)/shard_map/ppermute | solution.py:664
  12.6 2.6 %collective-permute-start.3 = (bf16[12,1664]{1,0:T(8,128)(2,1)S(1)}, bf16[12,1664]{1,0:T(8,128)(2,1)S(1)}, u32[]{:S(2)}, u32[]{:S(2)}) collective-permute-start(bf16[12,1664]{1,0:T(8,128)(2,1)S(1)} %get-tuple-element.143.refs_0_), channel_id=1, source_target_pairs={{0,16},{1,17},{2,18},{3,19},{4,20},{5,21},{6,22},{7,23},{8,24},{9,... | collective-permute-start | bytes 119816 | tf_op jit(solution)/shard_map/ppermute | solution.py:664
  15.2 1.1 quarter.1.near_one
  16.3 2.1 %collective-permute-done.refs_1_ = bf16[12,1664]{1,0:T(8,128)(2,1)S(1)} collective-permute-done((bf16[12,1664]{1,0:T(8,128)(2,1)S(1)}, bf16[12,1664]{1,0:T(8,128)(2,1)S(1)}, u32[]{:S(2)}, u32[]{:S(2)}) %collective-permute-start) | collective-permute-done | bytes 39968 | tf_op jit(solution)/shard_map/ppermute | solution.py:664
  18.4 1.2 collective-permute-done.3.refs_2_
  19.6 1.7 %collective-permute-done.4.refs_3_ = bf16[12,1664]{1,0:T(8,128)(2,1)S(1)} collective-permute-done((bf16[12,1664]{1,0:T(8,128)(2,1)S(1)}, bf16[12,1664]{1,0:T(8,128)(2,1)S(1)}, u32[]{:S(2)}, u32[]{:S(2)}) %collective-permute-start.4) | collective-permute-done | bytes 39968 | tf_op jit(solution)/shard_map/ppermute | solution.py:664
  22.4 2.5 %collective-permute-start.5 = (bf16[48,1664]{1,0:T(8,128)(2,1)S(1)}, bf16[48,1664]{1,0:T(8,128)(2,1)S(1)}, u32[]{:S(2)}, u32[]{:S(2)}) collective-permute-start(bf16[48,1664]{1,0:T(8,128)(2,1)S(1)} %join.2.refs_0_), channel_id=1, source_target_pairs={{0,2},{1,3},{2,0},{3,1},{4,6},{5,7},{6,4},{7,5},{8,10},{9,11},{10,... | collective-permute-start | bytes 479240 | tf_op jit(solution)/shard_map/ppermute | solution.py:664
  24.9 2.8 %collective-permute-done.7.refs_3_ = bf16[48,1664]{1,0:T(8,128)(2,1)S(1)} collective-permute-done((bf16[48,1664]{1,0:T(8,128)(2,1)S(1)}, bf16[48,1664]{1,0:T(8,128)(2,1)S(1)}, u32[]{:S(2)}, u32[]{:S(2)}) %collective-permute-start.7) | collective-permute-done | bytes 159776 | tf_op jit(solution)/shard_map/ppermute | solution.py:664
  27.6 1.2 collective-permute-done.6.refs_2_
  29.5 1.3 collective-permute-start.11
  30.8 1.7 %prepare.1 = (f32[1024,384]{1,0:T(8,128)S(1)}, f32[1024,128]{1,0:T(8,128)S(1)}, bf16[384,384]{1,0:T(8,128)(2,1)S(1)}, f32[1024,128]{1,0:T(8,128)S(1)}, f32[8,102...) custom-call(bf16[512,512]{1,0:T(8,128)(2,1)S(1)} %get-tuple-element.141.own, ...), custom_call_target="tpu_custom_call" | custom-call | flops 301989888 | bytes 1024 | tf_op jit(solution)/shard_map/prepare/pallas_call | solution.py:40
  32.5 7.5 %forward.1 = (bf16[640,768]{1,0:T(8,128)(2,1)S(1)}, bf16[160,768]{1,0:T(8,128)(2,1)S(1)}, bf16[160,768]{1,0:T(8,128)(2,1)S(1)}, bf16[160,768]{1,0:T(8,128)(2,1)S...) custom-call(f32[1024,384]{1,0:T(8,128)S(1)} %get-tuple-element.149.x, ...), custom_call_target="tpu_custom_call" | custom-call | bytes 1024 | tf_op jit(solution)/shard_map/forward/pallas_call | solution.py:40
  43.4 1.3 collective-permute-start.18
  44.7 5.0 %collective-permute-done.10.whole = bf16[768,384]{1,0:T(8,128)(2,1)S(1)} collective-permute-done((bf16[768,384]{1,0:T(8,128)(2,1)S(1)}, bf16[768,384]{1,0:T(8,128)(2,1)S(1)}, u32[]{:S(2)}, u32[]{:S(2)}) %collective-permute-start.10) | collective-permute-done | bytes 589856 | tf_op jit(solution)/shard_map/ppermute | solution.py:664
  49.7 1.1 collective-permute-start.16
  50.8 1.0 collective-permute-start.20
  51.8 1.0 collective-permute-start.19
  52.9 6.9 %collective-permute-done.16.refs_3_ = bf16[384,384]{1,0:T(8,128)(2,1)S(1)} collective-permute-done((bf16[384,384]{1,0:T(8,128)(2,1)S(1)}, bf16[384,384]{1,0:T(8,128)(2,1)S(1)}, u32[]{:S(2)}, u32[]{:S(2)}) %collective-permute-start.16) | collective-permute-done | bytes 294944 | tf_op jit(solution)/shard_map/ppermute | solution.py:664
  60.2 5.9 %collective-permute-done.20.refs_2_ = bf16[384,384]{1,0:T(8,128)(2,1)S(1)} collective-permute-done((bf16[384,384]{1,0:T(8,128)(2,1)S(1)}, bf16[384,384]{1,0:T(8,128)(2,1)S(1)}, u32[]{:S(2)}, u32[]{:S(2)}) %collective-permute-start.20) | collective-permute-done | bytes 294944 | tf_op jit(solution)/shard_map/ppermute | solution.py:664
  66.1 4.6 %collective-permute-done.19.near_out = bf16[384,384]{1,0:T(8,128)(2,1)S(1)} collective-permute-done((bf16[384,384]{1,0:T(8,128)(2,1)S(1)}, bf16[384,384]{1,0:T(8,128)(2,1)S(1)}, u32[]{:S(2)}, u32[]{:S(2)}) %collective-permute-start.19) | collective-permute-done | bytes 294944 | tf_op jit(solution)/shard_map/ppermute | solution.py:664
  74.0 5.6 %expert.3 = (bf16[320,768]{1,0:T(8,128)(2,1)S(1)}, bf16[320,768]{1,0:T(8,128)(2,1)S(1)}, bf16[640,1536]{1,0:T(8,128)(2,1)S(1)}, bf16[640,1536]{1,0:T(8,128)(2,1)S(1)}) custom-call(bf16[320,768]{1,0:T(8,128)(2,1)S(1)} %collective-permute-done.18.refs_0_.refs_2_, bf16[320,768]{1,0:T(8,128)(2,1)S(1)} %collective-permute-done.25.refs_1_.refs_3_, ...), custom_call_target="tpu_custom_call" | custom-call | flops 3019898880 | bytes 1024 | tf_op jit(solution)/shard_map/expert/pallas_call | solution.py:40
  79.6 5.5 %expert.2 = (bf16[320,768]{1,0:T(8,128)(2,1)S(1)}, bf16[320,768]{1,0:T(8,128)(2,1)S(1)}, bf16[640,1536]{1,0:T(8,128)(2,1)S(1)}, bf16[640,1536]{1,0:T(8,128)(2,1)S(1)}) custom-call(bf16[320,768]{1,0:T(8,128)(2,1)S(1)} %get-tuple-element.180.refs_0_, bf16[320,768]{1,0:T(8,128)(2,1)S(1)} %collective-permute-done.17.refs_1_, ...), custom_call_target="tpu_custom_call" | custom-call | flops 3019898880 | bytes 1024 | tf_op jit(solution)/shard_map/expert/pallas_call | solution.py:40
  85.1 4.0 %expert_grad.1 = (bf16[1536,384]{1,0:T(8,128)(2,1)S(1)}, bf16[1536,384]{1,0:T(8,128)(2,1)S(1)}) custom-call(bf16[320,768]{1,0:T(8,128)(2,1)S(1)} %get-tuple-element.180.refs_0_, bf16[320,768]{1,0:T(8,128)(2,1)S(1)} %collective-permute-done.17.refs_1_, bf16[320,768]{1,0:T(8,128)(2,1)S(1)} %collective-permute-done.18.refs_0_.refs_2_, ...), custom_call_target="tpu_custom_call" | custom-call | flops 3019898880 | bytes 1024 | tf_op jit(solution)/shard_map/expert_grad/pallas_call | solution.py:40
  89.9 3.0 %collective-permute-start.28 = (bf16[320,768]{1,0:T(8,128)(2,1)S(1)}, bf16[320,768]{1,0:T(8,128)(2,1)S(1)}, u32[]{:S(2)}, u32[]{:S(2)}) collective-permute-start(bf16[320,768]{1,0:T(8,128)(2,1)S(1)} %get-tuple-element.210), channel_id=1, source_target_pairs={{0,8},{1,9},{2,10},{3,11},{4,12},{5,13},{6,14},{7,15},{8,0},{9,1},... | collective-permute-start | bytes 1474568 | tf_op jit(solution)/shard_map/ppermute | solution.py:664
  92.8 1.0 split.1
  93.9 0.7 collective-permute-start.30
  94.6 1.4 collective-permute-start.31
  96.0 17.4 %collective-permute-done.27.refs_1_ = bf16[320,768]{1,0:T(8,128)(2,1)S(1)} collective-permute-done((bf16[320,768]{1,0:T(8,128)(2,1)S(1)}, bf16[320,768]{1,0:T(8,128)(2,1)S(1)}, u32[]{:S(2)}, u32[]{:S(2)}) %collective-permute-start.27) | collective-permute-done | bytes 491552 | tf_op jit(solution)/shard_map/ppermute | solution.py:664
  113.5 1.1 collective-permute-done.28.refs_2_
  116.5 1.4 collective-permute-start.41
  117.9 5.1 %combine.1 = (bf16[512,384]{1,0:T(8,128)(2,1)}, f32[512,384]{1,0:T(8,128)S(1)}, bf16[512,384]{1,0:T(8,128)(2,1)S(1)}, bf16[384,512]{1,0:T(8,128)(2,1)S(1)}) custom-call(f32[512,384]{1,0:T(8,128)S(1)} %get-tuple-element.163.middle, bf16[512,384]{1,0:T(8,128)(2,1)S(1)} %get-tuple-element.164.normed_two, f32[512,128]{1,0:T(8,128)S(1)} %get-tuple-element.165.probs, ...), custom_call_target="tpu_custom_call" | custom-call | flops 1509949440 | bytes 1024 | tf_op jit(solution)/shard_map/combine/pallas_call | solution.py:40
  123.0 9.5 %backward.1 = (bf16[512,384]{1,0:T(8,128)(2,1)S(1)}, bf16[256,768]{1,0:T(8,128)(2,1)S(1)}, bf16[256,768]{1,0:T(8,128)(2,1)S(1)}, f32[512,768]{1,0:T(8,128)S(1)},...) custom-call(bf16[1024,1152]{1,0:T(8,128)(2,1)S(1)} %get-tuple-elemen, ...), custom_call_target="tpu_custom_call" | custom-call | bytes 1024 | tf_op jit(solution)/shard_map/backward/pallas_call | solution.py:40
  134.8 0.9 collective-permute-start.42
  135.7 1.3 collective-permute-start.43
  137.0 1.4 collective-permute-start.44
  138.4 3.4 %collective-permute-done.42.refs_0_ = bf16[48,1664]{1,0:T(8,128)(2,1)S(1)} collective-permute-done((bf16[48,1664]{1,0:T(8,128)(2,1)S(1)}, bf16[48,1664]{1,0:T(8,128)(2,1)S(1)}, u32[]{:S(2)}, u32[]{:S(2)}) %collective-permute-start.42) | collective-permute-done | bytes 159776 | tf_op jit(solution)/shard_map/ppermute | solution.py:664
  141.8 3.3 %collective-permute-done.43.refs_1_ = bf16[48,1664]{1,0:T(8,128)(2,1)S(1)} collective-permute-done((bf16[48,1664]{1,0:T(8,128)(2,1)S(1)}, bf16[48,1664]{1,0:T(8,128)(2,1)S(1)}, u32[]{:S(2)}, u32[]{:S(2)}) %collective-permute-start.43) | collective-permute-done | bytes 159776 | tf_op jit(solution)/shard_map/ppermute | solution.py:664
  145.2 1.9 %collective-permute-start.47 = (bf16[256,768]{1,0:T(8,128)(2,1)S(1)}, bf16[256,768]{1,0:T(8,128)(2,1)S(1)}, u32[]{:S(2)}, u32[]{:S(2)}) collective-permute-start(bf16[256,768]{1,0:T(8,128)(2,1)S(1)} %get-tuple-element.252), channel_id=1, source_target_pairs={{0,1},{1,2},{2,3},{3,4},{4,5},{5,6},{6,7},{7,8},{8,9},{9,10},{10,1... | collective-permute-start | bytes 1179656 | tf_op jit(solution)/shard_map/ppermute | solution.py:951
  147.0 1.3 collective-permute-start.48
  148.4 6.7 %collective-permute-start.46 = (bf16[12,1664]{1,0:T(8,128)(2,1)S(1)}, bf16[12,1664]{1,0:T(8,128)(2,1)S(1)}, u32[]{:S(2)}, u32[]{:S(2)}) collective-permute-start(bf16[12,1664]{1,0:T(8,128)(2,1)S(1)} %get-tuple-element.249), channel_id=1, source_target_pairs={{0,8},{1,9},{2,10},{3,11},{4,12},{5,13},{6,14},{7,15},{8,0},{9,1},... | collective-permute-start | bytes 119816 | tf_op jit(solution)/shard_map/ppermute | solution.py:664
  155.5 2.1 %collective-permute-start.50 = (bf16[12,1664]{1,0:T(8,128)(2,1)S(1)}, bf16[12,1664]{1,0:T(8,128)(2,1)S(1)}, u32[]{:S(2)}, u32[]{:S(2)}) collective-permute-start(bf16[12,1664]{1,0:T(8,128)(2,1)S(1)} %get-tuple-element.261), channel_id=1, source_target_pairs={{0,24},{1,25},{2,26},{3,27},{4,28},{5,29},{6,30},{7,31},{8,16},{9,... | collective-permute-start | bytes 119816 | tf_op jit(solution)/shard_map/ppermute | solution.py:664
  157.6 2.4 %finish.1 = bf16[512,384]{1,0:T(8,128)(2,1)} custom-call(bf16[512,384]{1,0:T(8,128)(2,1)S(1)} %get-tuple-element.250.dq, f32[512,768]{1,0:T(8,128)S(1)} %get-tuple-element.251.inner, bf16[256,768]{1,0:T(8,128)(2,1)S(1)} %collective-permute-done.47.from_low, bf16[256,768]{1,0:T(8,128)(2,1)S(1)} %collective-permute-done.48.from_high, ...), custom_call_target="tpu_custom_call" | custom-call | flops 754974720 | bytes 1024 | tf_op jit(solution)/shard_map/finish/pallas_call | solution.py:40
  160.0 1.9 %collective-permute-done.46.refs_0_ = bf16[12,1664]{1,0:T(8,128)(2,1)S(1)} collective-permute-done((bf16[12,1664]{1,0:T(8,128)(2,1)S(1)}, bf16[12,1664]{1,0:T(8,128)(2,1)S(1)}, u32[]{:S(2)}, u32[]{:S(2)}) %collective-permute-start.46) | collective-permute-done | bytes 39968 | tf_op jit(solution)/shard_map/ppermute | solution.py:664
  161.9 2.1 %collective-permute-done.49.refs_1_ = bf16[12,1664]{1,0:T(8,128)(2,1)S(1)} collective-permute-done((bf16[12,1664]{1,0:T(8,128)(2,1)S(1)}, bf16[12,1664]{1,0:T(8,128)(2,1)S(1)}, u32[]{:S(2)}, u32[]{:S(2)}) %collective-permute-start.49) | collective-permute-done | bytes 39968 | tf_op jit(solution)/shard_map/ppermute | solution.py:664
  164.0 1.3 final.1
  (91 shorter events, 14.5 us)
Async XLA Ops:
  2.1 16.3 %collective-permute-start.1 = (bf16[256,512]{1,0:T(8,128)(2,1)S(1)}, bf16[256,512]{1,0:T(8,128)(2,1)S(1)}, u32[]{:S(2)}, u32[]{:S(2)}) collective-permute-start(bf16[256,512]{1,0:T(8,128)(2,1)S(1)} %get-tuple-element.144), channel_id=1, source_target_pairs={{0,1},{1,2},{2,3},{3,4},{4,5},{5,6},{6,7},{7,8},{8,9},{9,10},{10,1... | collective-permute-start | bytes 786440 | tf_op jit(solution)/shard_map/ppermute | solution.py:736
  4.5 13.9 %collective-permute-start.2 = (bf16[256,512]{1,0:T(8,128)(2,1)S(1)}, bf16[256,512]{1,0:T(8,128)(2,1)S(1)}, u32[]{:S(2)}, u32[]{:S(2)}) collective-permute-start(bf16[256,512]{1,0:T(8,128)(2,1)S(1)} %get-tuple-element.145), channel_id=1, source_target_pairs={{1,0},{2,1},{3,2},{4,3},{5,4},{6,5},{7,6},{8,7},{9,8},{10,9},{11,1... | collective-permute-start | bytes 786440 | tf_op jit(solution)/shard_map/ppermute | solution.py:737
  5.8 12.6 %collective-permute-start = (bf16[12,1664]{1,0:T(8,128)(2,1)S(1)}, bf16[12,1664]{1,0:T(8,128)(2,1)S(1)}, u32[]{:S(2)}, u32[]{:S(2)}) collective-permute-start(bf16[12,1664]{1,0:T(8,128)(2,1)S(1)} %get-tuple-element.143.refs_0_), channel_id=1, source_target_pairs={{0,8},{1,9},{2,10},{3,11},{4,12},{5,13},{6,14},{7,15},{8,0},{9,1},... | collective-permute-start | bytes 119816 | tf_op jit(solution)/shard_map/ppermute | solution.py:664
  12.6 7.0 %collective-permute-start.3 = (bf16[12,1664]{1,0:T(8,128)(2,1)S(1)}, bf16[12,1664]{1,0:T(8,128)(2,1)S(1)}, u32[]{:S(2)}, u32[]{:S(2)}) collective-permute-start(bf16[12,1664]{1,0:T(8,128)(2,1)S(1)} %get-tuple-element.143.refs_0_), channel_id=1, source_target_pairs={{0,16},{1,17},{2,18},{3,19},{4,20},{5,21},{6,22},{7,23},{8,24},{9,... | collective-permute-start | bytes 119816 | tf_op jit(solution)/shard_map/ppermute | solution.py:664
  15.2 6.1 %collective-permute-start.4 = (bf16[12,1664]{1,0:T(8,128)(2,1)S(1)}, bf16[12,1664]{1,0:T(8,128)(2,1)S(1)}, u32[]{:S(2)}, u32[]{:S(2)}) collective-permute-start(bf16[12,1664]{1,0:T(8,128)(2,1)S(1)} %get-tuple-element.143.refs_0_), channel_id=1, source_target_pairs={{0,24},{1,25},{2,26},{3,27},{4,28},{5,29},{6,30},{7,31},{8,16},{9,... | collective-permute-start | bytes 119816 | tf_op jit(solution)/shard_map/ppermute | solution.py:664
  21.3 6.3 %collective-permute-start.7 = (bf16[48,1664]{1,0:T(8,128)(2,1)S(1)}, bf16[48,1664]{1,0:T(8,128)(2,1)S(1)}, u32[]{:S(2)}, u32[]{:S(2)}) collective-permute-start(bf16[48,1664]{1,0:T(8,128)(2,1)S(1)} %join.2.refs_0_), channel_id=1, source_target_pairs={{0,6},{1,7},{2,4},{3,5},{4,2},{5,3},{6,0},{7,1},{8,14},{9,15},{10,... | collective-permute-start | bytes 479240 | tf_op jit(solution)/shard_map/ppermute | solution.py:664
  21.9 7.0 %collective-permute-start.6 = (bf16[48,1664]{1,0:T(8,128)(2,1)S(1)}, bf16[48,1664]{1,0:T(8,128)(2,1)S(1)}, u32[]{:S(2)}, u32[]{:S(2)}) collective-permute-start(bf16[48,1664]{1,0:T(8,128)(2,1)S(1)} %join.2.refs_0_), channel_id=1, source_target_pairs={{0,4},{1,5},{2,6},{3,7},{4,0},{5,1},{6,2},{7,3},{8,12},{9,13},{10,... | collective-permute-start | bytes 479240 | tf_op jit(solution)/shard_map/ppermute | solution.py:664
  22.4 6.5 %collective-permute-start.5 = (bf16[48,1664]{1,0:T(8,128)(2,1)S(1)}, bf16[48,1664]{1,0:T(8,128)(2,1)S(1)}, u32[]{:S(2)}, u32[]{:S(2)}) collective-permute-start(bf16[48,1664]{1,0:T(8,128)(2,1)S(1)} %join.2.refs_0_), channel_id=1, source_target_pairs={{0,2},{1,3},{2,0},{3,1},{4,6},{5,7},{6,4},{7,5},{8,10},{9,11},{10,... | collective-permute-start | bytes 479240 | tf_op jit(solution)/shard_map/ppermute | solution.py:664
  24.8 24.8 %collective-permute-start.10 = (bf16[768,384]{1,0:T(8,128)(2,1)S(1)}, bf16[768,384]{1,0:T(8,128)(2,1)S(1)}, u32[]{:S(2)}, u32[]{:S(2)}) collective-permute-start(bf16[768,384]{1,0:T(8,128)(2,1)S(1)} %quarter.1.near_one), channel_id=1, source_target_pairs={{0,16},{1,17},{2,18},{3,19},{4,20},{5,21},{6,22},{7,23},{8,24},{9,... | collective-permute-start | bytes 1769480 | tf_op jit(solution)/shard_map/ppermute | solution.py:664
  28.9 3.5 %collective-permute-start.8 = (bf16[96,1664]{1,0:T(8,128)(2,1)S(1)}, bf16[96,1664]{1,0:T(8,128)(2,1)S(1)}, u32[]{:S(2)}, u32[]{:S(2)}) collective-permute-start(bf16[96,1664]{1,0:T(8,128)(2,1)S(1)} %get-tuple-element.161.near_one), channel_id=1, source_target_pairs={{0,1},{1,0},{2,3},{3,2},{4,5},{5,4},{6,7},{7,6},{8,9},{9,8},{10,11... | collective-permute-start | bytes 958472 | tf_op jit(solution)/shard_map/ppermute | solution.py:664
  29.0 3.5 %collective-permute-start.9 = (bf16[96,1664]{1,0:T(8,128)(2,1)S(1)}, bf16[96,1664]{1,0:T(8,128)(2,1)S(1)}, u32[]{:S(2)}, u32[]{:S(2)}) collective-permute-start(bf16[96,1664]{1,0:T(8,128)(2,1)S(1)} %get-tuple-element.162.near_two), channel_id=1, source_target_pairs={{0,1},{1,0},{2,3},{3,2},{4,5},{5,4},{6,7},{7,6},{8,9},{9,8},{10,11... | collective-permute-start | bytes 958472 | tf_op jit(solution)/shard_map/ppermute | solution.py:664
  29.5 10.5 %collective-permute-start.11 = (bf16[384,384]{1,0:T(8,128)(2,1)S(1)}, bf16[384,384]{1,0:T(8,128)(2,1)S(1)}, u32[]{:S(2)}, u32[]{:S(2)}) collective-permute-start(bf16[384,384]{1,0:T(8,128)(2,1)S(1)} %bitcast.15), channel_id=1, source_target_pairs={{0,2},{1,3},{2,0},{3,1},{4,6},{5,7},{6,4},{7,5},{8,10},{9,11},{10,... | collective-permute-start | bytes 884744 | tf_op jit(solution)/shard_map/ppermute | solution.py:664
  40.0 1.6 collective-permute-start.12
  40.1 1.9 %collective-permute-start.13 = (bf16[160,768]{1,0:T(8,128)(2,1)S(1)}, bf16[160,768]{1,0:T(8,128)(2,1)S(1)}, u32[]{:S(2)}, u32[]{:S(2)}) collective-permute-start(bf16[160,768]{1,0:T(8,128)(2,1)S(1)} %get-tuple-element.176), channel_id=1, source_target_pairs={{0,1},{1,0},{2,3},{3,2},{4,5},{5,4},{6,7},{7,6},{8,9},{9,8},{10,11... | collective-permute-start | bytes 737288 | tf_op jit(solution)/shard_map/ppermute | solution.py:664
  40.6 1.7 %collective-permute-start.14 = (bf16[160,768]{1,0:T(8,128)(2,1)S(1)}, bf16[160,768]{1,0:T(8,128)(2,1)S(1)}, u32[]{:S(2)}, u32[]{:S(2)}) collective-permute-start(bf16[160,768]{1,0:T(8,128)(2,1)S(1)} %get-tuple-element.177), channel_id=1, source_target_pairs={{0,1},{1,0},{2,3},{3,2},{4,5},{5,4},{6,7},{7,6},{8,9},{9,8},{10,11... | collective-permute-start | bytes 737288 | tf_op jit(solution)/shard_map/ppermute | solution.py:664
  40.7 2.0 %collective-permute-start.15 = (bf16[160,768]{1,0:T(8,128)(2,1)S(1)}, bf16[160,768]{1,0:T(8,128)(2,1)S(1)}, u32[]{:S(2)}, u32[]{:S(2)}) collective-permute-start(bf16[160,768]{1,0:T(8,128)(2,1)S(1)} %get-tuple-element.178), channel_id=1, source_target_pairs={{0,1},{1,0},{2,3},{3,2},{4,5},{5,4},{6,7},{7,6},{8,9},{9,8},{10,11... | collective-permute-start | bytes 737288 | tf_op jit(solution)/shard_map/ppermute | solution.py:664
  42.8 17.0 %collective-permute-start.17 = (bf16[320,768]{1,0:T(8,128)(2,1)S(1)}, bf16[320,768]{1,0:T(8,128)(2,1)S(1)}, u32[]{:S(2)}, u32[]{:S(2)}) collective-permute-start(bf16[320,768]{1,0:T(8,128)(2,1)S(1)} %get-tuple-element.183), channel_id=1, source_target_pairs={{0,4},{1,5},{2,6},{3,7},{4,0},{5,1},{6,2},{7,3},{8,12},{9,13},{10,... | collective-permute-start | bytes 1474568 | tf_op jit(solution)/shard_map/ppermute | solution.py:664
  43.4 16.8 %collective-permute-start.18 = (bf16[320,768]{1,0:T(8,128)(2,1)S(1)}, bf16[320,768]{1,0:T(8,128)(2,1)S(1)}, u32[]{:S(2)}, u32[]{:S(2)}) collective-permute-start(bf16[320,768]{1,0:T(8,128)(2,1)S(1)} %get-tuple-element.184), channel_id=1, source_target_pairs={{0,8},{1,9},{2,10},{3,11},{4,12},{5,13},{6,14},{7,15},{8,0},{9,1},... | collective-permute-start | bytes 1474568 | tf_op jit(solution)/shard_map/ppermute | solution.py:664
  49.7 10.0 %collective-permute-start.16 = (bf16[384,384]{1,0:T(8,128)(2,1)S(1)}, bf16[384,384]{1,0:T(8,128)(2,1)S(1)}, u32[]{:S(2)}, u32[]{:S(2)}) collective-permute-start(bf16[384,384]{1,0:T(8,128)(2,1)S(1)} %get-tuple-element.182.refs_1_), channel_id=1, source_target_pairs={{0,2},{1,3},{2,0},{3,1},{4,6},{5,7},{6,4},{7,5},{8,10},{9,11},{10,... | collective-permute-start | bytes 884744 | tf_op jit(solution)/shard_map/ppermute | solution.py:664
  50.8 15.2 %collective-permute-start.20 = (bf16[384,384]{1,0:T(8,128)(2,1)S(1)}, bf16[384,384]{1,0:T(8,128)(2,1)S(1)}, u32[]{:S(2)}, u32[]{:S(2)}) collective-permute-start(bf16[384,384]{1,0:T(8,128)(2,1)S(1)} %get-tuple-element.188.refs_0_), channel_id=1, source_target_pairs={{0,2},{1,3},{2,0},{3,1},{4,6},{5,7},{6,4},{7,5},{8,10},{9,11},{10,... | collective-permute-start | bytes 884744 | tf_op jit(solution)/shard_map/ppermute | solution.py:664
  51.8 18.8 %collective-permute-start.19 = (bf16[384,384]{1,0:T(8,128)(2,1)S(1)}, bf16[384,384]{1,0:T(8,128)(2,1)S(1)}, u32[]{:S(2)}, u32[]{:S(2)}) collective-permute-start(bf16[384,384]{1,0:T(8,128)(2,1)S(1)} %bitcast.16), channel_id=1, source_target_pairs={{0,2},{1,3},{2,0},{3,1},{4,6},{5,7},{6,4},{7,5},{8,10},{9,11},{10,... | collective-permute-start | bytes 884744 | tf_op jit(solution)/shard_map/ppermute | solution.py:664
  59.7 12.4 %collective-permute-start.25 = (bf16[320,768]{1,0:T(8,128)(2,1)S(1)}, bf16[320,768]{1,0:T(8,128)(2,1)S(1)}, u32[]{:S(2)}, u32[]{:S(2)}) collective-permute-start(bf16[320,768]{1,0:T(8,128)(2,1)S(1)} %get-tuple-element.197), channel_id=1, source_target_pairs={{0,12},{1,13},{2,14},{3,15},{4,8},{5,9},{6,10},{7,11},{8,4},{9,5},... | collective-permute-start | bytes 1474568 | tf_op jit(solution)/shard_map/ppermute | solution.py:664
  71.1 1.6 collective-permute-start.21
  71.1 2.0 %collective-permute-start.22 = (bf16[384,384]{1,0:T(8,128)(2,1)S(1)}, bf16[384,384]{1,0:T(8,128)(2,1)S(1)}, u32[]{:S(2)}, u32[]{:S(2)}) collective-permute-start(bf16[384,384]{1,0:T(8,128)(2,1)S(1)} %get-tuple-element.192), channel_id=1, source_target_pairs={{0,1},{1,0},{2,3},{3,2},{4,5},{5,4},{6,7},{7,6},{8,9},{9,8},{10,11... | collective-permute-start | bytes 884744 | tf_op jit(solution)/shard_map/ppermute | solution.py:664
  71.6 1.9 %collective-permute-start.23 = (bf16[384,384]{1,0:T(8,128)(2,1)S(1)}, bf16[384,384]{1,0:T(8,128)(2,1)S(1)}, u32[]{:S(2)}, u32[]{:S(2)}) collective-permute-start(bf16[384,384]{1,0:T(8,128)(2,1)S(1)} %get-tuple-element.193), channel_id=1, source_target_pairs={{0,1},{1,0},{2,3},{3,2},{4,5},{5,4},{6,7},{7,6},{8,9},{9,8},{10,11... | collective-permute-start | bytes 884744 | tf_op jit(solution)/shard_map/ppermute | solution.py:664
  71.7 2.3 %collective-permute-start.24 = (bf16[384,384]{1,0:T(8,128)(2,1)S(1)}, bf16[384,384]{1,0:T(8,128)(2,1)S(1)}, u32[]{:S(2)}, u32[]{:S(2)}) collective-permute-start(bf16[384,384]{1,0:T(8,128)(2,1)S(1)} %get-tuple-element.194), channel_id=1, source_target_pairs={{0,1},{1,0},{2,3},{3,2},{4,5},{5,4},{6,7},{7,6},{8,9},{9,8},{10,11... | collective-permute-start | bytes 884744 | tf_op jit(solution)/shard_map/ppermute | solution.py:664
  89.1 3.7 %collective-permute-start.26 = (bf16[1536,384]{1,0:T(8,128)(2,1)S(1)}, bf16[1536,384]{1,0:T(8,128)(2,1)S(1)}, u32[]{:S(2)}, u32[]{:S(2)}) collective-permute-start(bf16[1536,384]{1,0:T(8,128)(2,1)S(1)} %get-tuple-element.203), channel_id=1, source_target_pairs={{0,1},{1,0},{2,3},{3,2},{4,5},{5,4},{6,7},{7,6},{8,9},{9,8},{10,11... | collective-permute-start | bytes 3538952 | tf_op jit(solution)/shard_map/ppermute | solution.py:664
  89.3 24.0 %collective-permute-start.27 = (bf16[320,768]{1,0:T(8,128)(2,1)S(1)}, bf16[320,768]{1,0:T(8,128)(2,1)S(1)}, u32[]{:S(2)}, u32[]{:S(2)}) collective-permute-start(bf16[320,768]{1,0:T(8,128)(2,1)S(1)} %get-tuple-element.208), channel_id=1, source_target_pairs={{0,4},{1,5},{2,6},{3,7},{4,0},{5,1},{6,2},{7,3},{8,12},{9,13},{10,... | collective-permute-start | bytes 1474568 | tf_op jit(solution)/shard_map/ppermute | solution.py:664
  89.9 23.7 %collective-permute-start.29 = (bf16[320,768]{1,0:T(8,128)(2,1)S(1)}, bf16[320,768]{1,0:T(8,128)(2,1)S(1)}, u32[]{:S(2)}, u32[]{:S(2)}) collective-permute-start(bf16[320,768]{1,0:T(8,128)(2,1)S(1)} %get-tuple-element.211), channel_id=1, source_target_pairs={{0,12},{1,13},{2,14},{3,15},{4,8},{5,9},{6,10},{7,11},{8,4},{9,5},... | collective-permute-start | bytes 1474568 | tf_op jit(solution)/shard_map/ppermute | solution.py:664
  89.9 24.7 %collective-permute-start.28 = (bf16[320,768]{1,0:T(8,128)(2,1)S(1)}, bf16[320,768]{1,0:T(8,128)(2,1)S(1)}, u32[]{:S(2)}, u32[]{:S(2)}) collective-permute-start(bf16[320,768]{1,0:T(8,128)(2,1)S(1)} %get-tuple-element.210), channel_id=1, source_target_pairs={{0,8},{1,9},{2,10},{3,11},{4,12},{5,13},{6,14},{7,15},{8,0},{9,1},... | collective-permute-start | bytes 1474568 | tf_op jit(solution)/shard_map/ppermute | solution.py:664
  93.9 19.5 %collective-permute-start.30 = (bf16[384,384]{1,0:T(8,128)(2,1)S(1)}, bf16[384,384]{1,0:T(8,128)(2,1)S(1)}, u32[]{:S(2)}, u32[]{:S(2)}) collective-permute-start(bf16[384,384]{1,0:T(8,128)(2,1)S(1)} %get-tuple-element.213), channel_id=1, source_target_pairs={{0,2},{1,3},{2,0},{3,1},{4,6},{5,7},{6,4},{7,5},{8,10},{9,11},{10,... | collective-permute-start | bytes 884744 | tf_op jit(solution)/shard_map/ppermute | solution.py:664
  94.6 18.8 %collective-permute-start.31 = (bf16[384,384]{1,0:T(8,128)(2,1)S(1)}, bf16[384,384]{1,0:T(8,128)(2,1)S(1)}, u32[]{:S(2)}, u32[]{:S(2)}) collective-permute-start(bf16[384,384]{1,0:T(8,128)(2,1)S(1)} %get-tuple-element.214), channel_id=1, source_target_pairs={{0,2},{1,3},{2,0},{3,1},{4,6},{5,7},{6,4},{7,5},{8,10},{9,11},{10,... | collective-permute-start | bytes 884744 | tf_op jit(solution)/shard_map/ppermute | solution.py:664
  114.7 1.8 %collective-permute-start.32 = (bf16[160,768]{1,0:T(8,128)(2,1)S(1)}, bf16[160,768]{1,0:T(8,128)(2,1)S(1)}, u32[]{:S(2)}, u32[]{:S(2)}) collective-permute-start(bf16[160,768]{1,0:T(8,128)(2,1)S(1)} %get-tuple-element.217), channel_id=1, source_target_pairs={{0,1},{1,0},{2,3},{3,2},{4,5},{5,4},{6,7},{7,6},{8,9},{9,8},{10,11... | collective-permute-start | bytes 737288 | tf_op jit(solution)/shard_map/ppermute | solution.py:664
  114.8 3.0 %collective-permute-start.33 = (bf16[160,768]{1,0:T(8,128)(2,1)S(1)}, bf16[160,768]{1,0:T(8,128)(2,1)S(1)}, u32[]{:S(2)}, u32[]{:S(2)}) collective-permute-start(bf16[160,768]{1,0:T(8,128)(2,1)S(1)} %get-tuple-element.218), channel_id=1, source_target_pairs={{0,1},{1,0},{2,3},{3,2},{4,5},{5,4},{6,7},{7,6},{8,9},{9,8},{10,11... | collective-permute-start | bytes 737288 | tf_op jit(solution)/shard_map/ppermute | solution.py:664
  115.3 2.6 %collective-permute-start.34 = (bf16[160,768]{1,0:T(8,128)(2,1)S(1)}, bf16[160,768]{1,0:T(8,128)(2,1)S(1)}, u32[]{:S(2)}, u32[]{:S(2)}) collective-permute-start(bf16[160,768]{1,0:T(8,128)(2,1)S(1)} %get-tuple-element.219), channel_id=1, source_target_pairs={{0,1},{1,0},{2,3},{3,2},{4,5},{5,4},{6,7},{7,6},{8,9},{9,8},{10,11... | collective-permute-start | bytes 737288 | tf_op jit(solution)/shard_map/ppermute | solution.py:664
  115.4 2.5 %collective-permute-start.35 = (bf16[160,768]{1,0:T(8,128)(2,1)S(1)}, bf16[160,768]{1,0:T(8,128)(2,1)S(1)}, u32[]{:S(2)}, u32[]{:S(2)}) collective-permute-start(bf16[160,768]{1,0:T(8,128)(2,1)S(1)} %get-tuple-element.220), channel_id=1, source_target_pairs={{0,1},{1,0},{2,3},{3,2},{4,5},{5,4},{6,7},{7,6},{8,9},{9,8},{10,11... | collective-permute-start | bytes 737288 | tf_op jit(solution)/shard_map/ppermute | solution.py:664
  115.8 17.3 %collective-permute-start.40 = (bf16[384,384]{1,0:T(8,128)(2,1)S(1)}, bf16[384,384]{1,0:T(8,128)(2,1)S(1)}, u32[]{:S(2)}, u32[]{:S(2)}) collective-permute-start(bf16[384,384]{1,0:T(8,128)(2,1)S(1)} %get-tuple-element.233), channel_id=1, source_target_pairs={{0,2},{1,3},{2,0},{3,1},{4,6},{5,7},{6,4},{7,5},{8,10},{9,11},{10,... | collective-permute-start | bytes 884744 | tf_op jit(solution)/shard_map/ppermute | solution.py:664
  116.5 16.7 %collective-permute-start.41 = (bf16[384,384]{1,0:T(8,128)(2,1)S(1)}, bf16[384,384]{1,0:T(8,128)(2,1)S(1)}, u32[]{:S(2)}, u32[]{:S(2)}) collective-permute-start(bf16[384,384]{1,0:T(8,128)(2,1)S(1)} %get-tuple-element.234), channel_id=1, source_target_pairs={{0,2},{1,3},{2,0},{3,1},{4,6},{5,7},{6,4},{7,5},{8,10},{9,11},{10,... | collective-permute-start | bytes 884744 | tf_op jit(solution)/shard_map/ppermute | solution.py:664
  117.8 27.3 %collective-permute-start.45 = (bf16[768,384]{1,0:T(8,128)(2,1)S(1)}, bf16[768,384]{1,0:T(8,128)(2,1)S(1)}, u32[]{:S(2)}, u32[]{:S(2)}) collective-permute-start(bf16[768,384]{1,0:T(8,128)(2,1)S(1)} %away.1), channel_id=1, source_target_pairs={{0,16},{1,17},{2,18},{3,19},{4,20},{5,21},{6,22},{7,23},{8,24},{9,... | collective-permute-start | bytes 1769480 | tf_op jit(solution)/shard_map/ppermute | solution.py:664
  132.6 1.6 collective-permute-start.37
  134.8 7.0 %collective-permute-start.42 = (bf16[48,1664]{1,0:T(8,128)(2,1)S(1)}, bf16[48,1664]{1,0:T(8,128)(2,1)S(1)}, u32[]{:S(2)}, u32[]{:S(2)}) collective-permute-start(bf16[48,1664]{1,0:T(8,128)(2,1)S(1)} %get-tuple-element.240), channel_id=1, source_target_pairs={{0,2},{1,3},{2,0},{3,1},{4,6},{5,7},{6,4},{7,5},{8,10},{9,11},{10,... | collective-permute-start | bytes 479240 | tf_op jit(solution)/shard_map/ppermute | solution.py:664
  135.7 9.4 %collective-permute-start.43 = (bf16[48,1664]{1,0:T(8,128)(2,1)S(1)}, bf16[48,1664]{1,0:T(8,128)(2,1)S(1)}, u32[]{:S(2)}, u32[]{:S(2)}) collective-permute-start(bf16[48,1664]{1,0:T(8,128)(2,1)S(1)} %get-tuple-element.241), channel_id=1, source_target_pairs={{0,4},{1,5},{2,6},{3,7},{4,0},{5,1},{6,2},{7,3},{8,12},{9,13},{10,... | collective-permute-start | bytes 479240 | tf_op jit(solution)/shard_map/ppermute | solution.py:664
  137.0 8.2 %collective-permute-start.44 = (bf16[48,1664]{1,0:T(8,128)(2,1)S(1)}, bf16[48,1664]{1,0:T(8,128)(2,1)S(1)}, u32[]{:S(2)}, u32[]{:S(2)}) collective-permute-start(bf16[48,1664]{1,0:T(8,128)(2,1)S(1)} %get-tuple-element.242), channel_id=1, source_target_pairs={{0,6},{1,7},{2,4},{3,5},{4,2},{5,3},{6,0},{7,1},{8,14},{9,15},{10,... | collective-permute-start | bytes 479240 | tf_op jit(solution)/shard_map/ppermute | solution.py:664
  145.2 12.5 %collective-permute-start.47 = (bf16[256,768]{1,0:T(8,128)(2,1)S(1)}, bf16[256,768]{1,0:T(8,128)(2,1)S(1)}, u32[]{:S(2)}, u32[]{:S(2)}) collective-permute-start(bf16[256,768]{1,0:T(8,128)(2,1)S(1)} %get-tuple-element.252), channel_id=1, source_target_pairs={{0,1},{1,2},{2,3},{3,4},{4,5},{5,6},{6,7},{7,8},{8,9},{9,10},{10,1... | collective-permute-start | bytes 1179656 | tf_op jit(solution)/shard_map/ppermute | solution.py:951
  147.0 10.6 %collective-permute-start.48 = (bf16[256,768]{1,0:T(8,128)(2,1)S(1)}, bf16[256,768]{1,0:T(8,128)(2,1)S(1)}, u32[]{:S(2)}, u32[]{:S(2)}) collective-permute-start(bf16[256,768]{1,0:T(8,128)(2,1)S(1)} %get-tuple-element.253), channel_id=1, source_target_pairs={{1,0},{2,1},{3,2},{4,3},{5,4},{6,5},{7,6},{8,7},{9,8},{10,9},{11,1... | collective-permute-start | bytes 1179656 | tf_op jit(solution)/shard_map/ppermute | solution.py:950
  148.4 13.4 %collective-permute-start.46 = (bf16[12,1664]{1,0:T(8,128)(2,1)S(1)}, bf16[12,1664]{1,0:T(8,128)(2,1)S(1)}, u32[]{:S(2)}, u32[]{:S(2)}) collective-permute-start(bf16[12,1664]{1,0:T(8,128)(2,1)S(1)} %get-tuple-element.249), channel_id=1, source_target_pairs={{0,8},{1,9},{2,10},{3,11},{4,12},{5,13},{6,14},{7,15},{8,0},{9,1},... | collective-permute-start | bytes 119816 | tf_op jit(solution)/shard_map/ppermute | solution.py:664
  155.2 8.8 %collective-permute-start.49 = (bf16[12,1664]{1,0:T(8,128)(2,1)S(1)}, bf16[12,1664]{1,0:T(8,128)(2,1)S(1)}, u32[]{:S(2)}, u32[]{:S(2)}) collective-permute-start(bf16[12,1664]{1,0:T(8,128)(2,1)S(1)} %get-tuple-element.260), channel_id=1, source_target_pairs={{0,16},{1,17},{2,18},{3,19},{4,20},{5,21},{6,22},{7,23},{8,24},{9,... | collective-permute-start | bytes 119816 | tf_op jit(solution)/shard_map/ppermute | solution.py:664
  155.5 8.4 %collective-permute-start.50 = (bf16[12,1664]{1,0:T(8,128)(2,1)S(1)}, bf16[12,1664]{1,0:T(8,128)(2,1)S(1)}, u32[]{:S(2)}, u32[]{:S(2)}) collective-permute-start(bf16[12,1664]{1,0:T(8,128)(2,1)S(1)} %get-tuple-element.261), channel_id=1, source_target_pairs={{0,24},{1,25},{2,26},{3,27},{4,28},{5,29},{6,30},{7,31},{8,16},{9,... | collective-permute-start | bytes 119816 | tf_op jit(solution)/shard_map/ppermute | solution.py:664
  (11 other events, 174.7 us)
where the time goes:
time: 165 us
  waiting for transfers between devices  65.5 us (40%)
  starting transfers between devices  51.5 us (31%)
  Pallas kernels  47.2 us (29%)
    ppermute x47, waiting for transfers between devices, swap(): return lax.ppermute(value, 'dp', [(i, i ^ mask) for i in range(devices)])  65.5 us
    pallas_call x21, Pallas kernels, call(): pl.pallas_call(body, out_shape=tuple(outs), in_specs=[spec] * len(ins), o...  47.2 us
    ppermute x47, starting transfers between devices, swap(): return lax.ppermute(value, 'dp', [(i, i ^ mask) for i in range(devices)])  44.6 us
  transfers between devices with their start and end apart: 51, of which 28 were waited for; matrix products, arithmetic and copies ran while one was open for 0% of the time, Pallas kernels for 18%

commit v1 on v0

--- a/solution.py
+++ b/solution.py
@@ -115,21 +115,40 @@
         out[...] = whole[index * size : (index + 1) * size, :]
 
 
+def normed_rows(ref, width, sel):
+    values = dot(ref[:, :width], sel)
+    centered = values - jnp.mean(values, axis=1, keepdims=True)
+    rstd = lax.rsqrt(jnp.mean(centered * centered, axis=1, keepdims=True) + EPSILON)
+    return centered * rstd, rstd
+
+
+def halo_body(width, own, low, high, select, xhat, idcol, idrow):
+    sel = select[...]
+    xhat[:HALO, :] = normed_rows(low, width, sel)[0]
+    xhat[HALO:, :] = normed_rows(high, width, sel)[0]
+    start = 0
+    for ref in (low, own, high):
+        rows = ref.shape[0]
+        marks = ref[:, width : width + LANES].astype(F32)
+        column = marks[:, 0:1] * 256.0 + marks[:, 1:2]
+        idcol[start : start + rows, :] = jnp.broadcast_to(column, (rows, LANES))
+        turned = marks.T
+        line = turned[0:1, :] * 256.0 + turned[1:2, :]
+        idrow[:, start : start + rows] = jnp.broadcast_to(line, (8, rows))
+        start += rows
+
+
 def prepare_body(
     width,
     experts,
     capacity,
     own,
-    low,
-    high,
     order,
     experts_row,
     slots_row,
     xhat,
     rstd_out,
     select,
-    idcol,
-    idrow,
     routes,
     place_row,
 ):
@@ -139,22 +158,8 @@
     target = (me ^ order[0:1, :]) * share + order[1:2, :]
     sel = (lax.broadcasted_iota(jnp.int32, (width, width), 0) == target).astype(F32).astype(BF)
     select[...] = sel
-    start = 0
-    for ref in (low, own, high):
-        rows = ref.shape[0]
-        values = dot(ref[:, :width], sel)
-        mean = jnp.mean(values, axis=1, keepdims=True)
-        centered = values - mean
-        rstd = lax.rsqrt(jnp.mean(centered * centered, axis=1, keepdims=True) + EPSILON)
-        xhat[start : start + rows, :] = centered * rstd
-        rstd_out[start : start + rows, :] = jnp.broadcast_to(rstd, (rows, LANES))
-        marks = ref[:, width : width + LANES].astype(F32)
-        column = marks[:, 0:1] * 256.0 + marks[:, 1:2]
-        idcol[start : start + rows, :] = jnp.broadcast_to(column, (rows, LANES))
-        turned = marks.T
-        line = turned[0:1, :] * 256.0 + turned[1:2, :]
-        idrow[:, start : start + rows] = jnp.broadcast_to(line, (8, rows))
-        start += rows
+    xhat[...], rstd = normed_rows(own, width, sel)
+    rstd_out[...] = jnp.broadcast_to(rstd, rstd_out.shape)
     rows = own.shape[0]
     group = (((me >> 2) & (experts // 2 - 1)) << 1) | (me & 1)
     half_bits = (experts // 2).bit_length() - 1
@@ -183,6 +188,7 @@
     experts,
     capacity,
     xhat,
+    xhat_halo,
     idcol,
     idrow,
     select,
@@ -199,7 +205,6 @@
     same_core, other_core, outs = outs[0], outs[1 : 1 + experts // 2], outs[1 + experts // 2 :]
     qkv, attended, lse, middle, normed_two, probs, normed, weights, weights_tail, gain = outs
     rows = own.shape[0]
-    span = xhat.shape[0]
     cols = 3 * width
     parts = (near_one, near_two, far_one, far_two)
     size = width // 4
@@ -212,7 +217,9 @@
     natural = dot(sel, tail)
     weights_tail[...] = natural.astype(BF)
     gain_two = natural[:, width:].T[experts + 1 : experts + 2, :]
-    normed[...] = (xhat[...] * gain_row).astype(BF)
+    normed[:HALO, :] = (xhat_halo[:HALO, :] * gain_row).astype(BF)
+    normed[HALO : HALO + rows, :] = (xhat[...] * gain_row).astype(BF)
+    normed[HALO + rows :, :] = (xhat_halo[HALO:, :] * gain_row).astype(BF)
     qkv[HALO : HALO + rows, :] = dot(normed[HALO : HALO + rows, :], weights[...]).astype(BF)
     for first in (0, HALO + rows):
         qkv[first : first + HALO, width:] = dot(
@@ -589,9 +596,9 @@
     values = dot(dq[...], weights[:, :width], 1, 1) + dot(
         grad[...].astype(BF), weights[:, width:], 1, 1
     )
-    hat = xhat[HALO : HALO + rows, :]
+    hat = xhat[...]
     values = values * normed_gain[0:1, :]
-    part = rstd[HALO : HALO + rows, 0:1] * (
+    part = rstd[:, 0:1] * (
         values
         - jnp.mean(values, axis=1, keepdims=True)
         - hat * jnp.mean(values * hat, axis=1, keepdims=True)
@@ -745,16 +752,37 @@
         fetch=True,
     )[0]
     order = [0]
+    for stage in stages:
+        order = [a ^ mask for mask in [0] + stage for a in order]
+    order = np.stack(
+        [
+            np.repeat(np.array(order, np.int32), share),
+            np.tile(np.arange(share, dtype=np.int32), devices),
+        ]
+    )
+    packed, own = lax.optimization_barrier((packed, own))
+    xhat, rstd, select, routes, place_row = call(
+        functools.partial(prepare_body, width, experts, capacity),
+        [
+            shape((rows, width), F32),
+            shape((rows, LANES), F32),
+            shape((width, width), BF),
+            shape((rows, LANES), F32),
+            shape((8, rows), F32),
+        ],
+        [own, jnp.asarray(order), expert_ids.T, slots.T],
+        name="prepare",
+    )
     near = [packed]
     far = None
     for stage in stages:
-        order = [a ^ mask for mask in [0] + stage for a in order]
         arrived = [swap(part, devices, mask) for mask in stage for part in near]
         if stage is stages[0]:
             arrived[0], low, high, quarter = lax.optimization_barrier(
                 (arrived[0], low, high, quarter)
             )
             arrived[1], quarter_far = lax.optimization_barrier((arrived[1], quarter))
+            arrived[2], xhat = lax.optimization_barrier((arrived[2], xhat))
         if stage is stages[-2]:
             *arrived, late_in = lax.optimization_barrier((*arrived, w_in[0]))
         if stage is stages[-1]:
@@ -768,13 +796,6 @@
                 [*near, *arrived],
                 name="join",
             )
-    order = np.stack(
-        [
-            np.repeat(np.array(order, np.int32), share),
-            np.tile(np.arange(share, dtype=np.int32), devices),
-        ]
-    )
-
     far_quarter = swap(quarter_far, devices, half)
     near_in = swap(late_in, devices, 2)
 
@@ -783,20 +804,15 @@
             swap(part, devices, 4 * index) for index, part in enumerate(parts) if index
         ]
 
-    xhat, rstd, select, idcol, idrow, routes, place_row = call(
-        functools.partial(prepare_body, width, experts, capacity),
+    xhat_halo, idcol, idrow = call(
+        functools.partial(halo_body, width),
         [
-            shape((span, width), F32),
-            shape((span, LANES), F32),
-            shape((width, width), BF),
+            shape((2 * HALO, width), F32),
             shape((span, LANES), F32),
             shape((8, span), F32),
-            shape((rows, LANES), F32),
-            shape((8, rows), F32),
         ],
-        [own, low, high, jnp.asarray(order), expert_ids.T, slots.T],
-        flops=2 * span * width * width,
-        name="prepare",
+        [own, low, high, select],
+        name="halo",
     )
     chips = experts // 2
     half_slots = chips * capacity
@@ -816,7 +832,7 @@
             shape((width, width + LANES), BF),
             shape((8, width), F32),
         ],
-        [xhat, idcol, idrow, select, own, cotangent, routes, place_row, *near, *far],
+        [xhat, xhat_halo, idcol, idrow, select, own, cotangent, routes, place_row, *near, *far],
         name="forward",
     )
     same_core, other_core, outs = outs[0], outs[1 : 1 + chips], outs[1 + chips :]

time: 165 us -> 166 us (level)
  starting transfers between devices: 51.5 us -> 54.5 us
  waiting for transfers between devices: 65.5 us -> 62.8 us
    ppermute x47, starting transfers between devices: 44.6 us -> 48 us  [swap(): return lax.ppermute(value, 'dp', [(i, i ^ mask) for i in range(devices)])]
    ppermute x47, waiting for transfers between devices: 65.5 us -> 62.8 us  [swap(): return lax.ppermute(value, 'dp', [(i, i ^ mask) for i in range(devices)])]
    pallas_call x21 -> x22, Pallas kernels: 47.2 us -> 47.3 us  [call(): pl.pallas_call(body, out_shape=tuple(outs), in_specs=[spec] * len(ins), o...]
  transfers between devices with their start and end apart: 51 -> 51, of which waited for: 28 -> 27; matrix products, arithmetic and copies ran while one was open for 0% -> 0% of each run, Pallas kernels for 18% -> 18%
where the time goes in v1:
time: 166 us
  waiting for transfers between devices  62.8 us (38%)
  starting transfers between devices  54.5 us (33%)
  Pallas kernels  47.3 us (28%)
    ppermute x47, waiting for transfers between devices, swap(): return lax.ppermute(value, 'dp', [(i, i ^ mask) for i in range(devices)])  62.8 us
    ppermute x47, starting transfers between devices, swap(): return lax.ppermute(value, 'dp', [(i, i ^ mask) for i in range(devices)])  48 us
    pallas_call x22, Pallas kernels, call(): pl.pallas_call(body, out_shape=tuple(outs), in_specs=[spec] * len(ins), o...  47.3 us
  transfers between devices with their start and end apart: 51, of which 27 were waited for; matrix products, arithmetic and copies ran while one was open for 0% of the time, Pallas kernels for 18%

profile of v1, /device:TPU:0, one launch (start us, length us, event | category | flops | bytes accessed | tf_op | source)
XLA Modules:
  0.0 165.7 jit_solution(4245685201920563213)
XLA Ops:
  0.7 1.4 pack.1
  2.1 2.4 %collective-permute-start.2 = (bf16[256,512]{1,0:T(8,128)(2,1)S(1)}, bf16[256,512]{1,0:T(8,128)(2,1)S(1)}, u32[]{:S(2)}, u32[]{:S(2)}) collective-permute-start(bf16[256,512]{1,0:T(8,128)(2,1)S(1)} %get-tuple-element.153), channel_id=1, source_target_pairs={{0,1},{1,2},{2,3},{3,4},{4,5},{5,6},{6,7},{7,8},{8,9},{9,10},{10,1... | collective-permute-start | bytes 786440 | tf_op jit(solution)/shard_map/ppermute | solution.py:743
  4.5 1.3 collective-permute-start.3
  5.8 8.8 %collective-permute-start = (bf16[12,1664]{1,0:T(8,128)(2,1)S(1)}, bf16[12,1664]{1,0:T(8,128)(2,1)S(1)}, u32[]{:S(2)}, u32[]{:S(2)}) collective-permute-start(bf16[12,1664]{1,0:T(8,128)(2,1)S(1)} %get-tuple-element.149.refs_0_), channel_id=1, source_target_pairs={{0,24},{1,25},{2,26},{3,27},{4,28},{5,29},{6,30},{7,31},{8,16},{9,... | collective-permute-start | bytes 119816 | tf_op jit(solution)/shard_map/ppermute | solution.py:671
  14.6 0.6 collective-permute-start.4
  15.3 1.1 quarter.1.near_one
  17.0 3.1 %collective-permute-done.refs_3_ = bf16[12,1664]{1,0:T(8,128)(2,1)S(1)} collective-permute-done((bf16[12,1664]{1,0:T(8,128)(2,1)S(1)}, bf16[12,1664]{1,0:T(8,128)(2,1)S(1)}, u32[]{:S(2)}, u32[]{:S(2)}) %collective-permute-start) | collective-permute-done | bytes 39968 | tf_op jit(solution)/shard_map/ppermute | solution.py:671
  20.1 1.1 collective-permute-done.4.refs_2_
  21.5 3.4 %collective-permute-start.5 = (bf16[48,1664]{1,0:T(8,128)(2,1)S(1)}, bf16[48,1664]{1,0:T(8,128)(2,1)S(1)}, u32[]{:S(2)}, u32[]{:S(2)}) collective-permute-start(bf16[48,1664]{1,0:T(8,128)(2,1)S(1)} %join.2.refs_0_), channel_id=1, source_target_pairs={{0,2},{1,3},{2,0},{3,1},{4,6},{5,7},{6,4},{7,5},{8,10},{9,11},{10,... | collective-permute-start | bytes 479240 | tf_op jit(solution)/shard_map/ppermute | solution.py:671
  24.9 2.8 %collective-permute-done.7.refs_3_ = bf16[48,1664]{1,0:T(8,128)(2,1)S(1)} collective-permute-done((bf16[48,1664]{1,0:T(8,128)(2,1)S(1)}, bf16[48,1664]{1,0:T(8,128)(2,1)S(1)}, u32[]{:S(2)}, u32[]{:S(2)}) %collective-permute-start.7) | collective-permute-done | bytes 159776 | tf_op jit(solution)/shard_map/ppermute | solution.py:671
  27.7 0.8 collective-permute-done.6.refs_2_
  29.1 1.7 %collective-permute-start.11 = (bf16[384,384]{1,0:T(8,128)(2,1)S(1)}, bf16[384,384]{1,0:T(8,128)(2,1)S(1)}, u32[]{:S(2)}, u32[]{:S(2)}) collective-permute-start(bf16[384,384]{1,0:T(8,128)(2,1)S(1)} %bitcast.15), channel_id=1, source_target_pairs={{0,2},{1,3},{2,0},{3,1},{4,6},{5,7},{6,4},{7,5},{8,10},{9,11},{10,... | collective-permute-start | bytes 884744 | tf_op jit(solution)/shard_map/ppermute | solution.py:671
  30.8 1.1 halo.1
  31.9 7.5 %forward.1 = (bf16[640,768]{1,0:T(8,128)(2,1)S(1)}, bf16[160,768]{1,0:T(8,128)(2,1)S(1)}, bf16[160,768]{1,0:T(8,128)(2,1)S(1)}, bf16[160,768]{1,0:T(8,128)(2,1)S...) custom-call(f32[512,384]{1,0:T(8,128)S(1)} %get-tuple-element.152.xh, ...), custom_call_target="tpu_custom_call" | custom-call | bytes 1024 | tf_op jit(solution)/shard_map/forward/pallas_call | solution.py:40
  42.2 0.8 collective-permute-start.17
  43.0 1.0 collective-permute-start.18
  44.1 5.2 %collective-permute-done.10.whole = bf16[768,384]{1,0:T(8,128)(2,1)S(1)} collective-permute-done((bf16[768,384]{1,0:T(8,128)(2,1)S(1)}, bf16[768,384]{1,0:T(8,128)(2,1)S(1)}, u32[]{:S(2)}, u32[]{:S(2)}) %collective-permute-start.10) | collective-permute-done | bytes 589856 | tf_op jit(solution)/shard_map/ppermute | solution.py:671
  49.4 1.5 collective-permute-start.16
  50.8 0.6 collective-permute-start.20
  51.5 1.4 collective-permute-start.19
  52.9 6.5 %collective-permute-done.16.refs_3_ = bf16[384,384]{1,0:T(8,128)(2,1)S(1)} collective-permute-done((bf16[384,384]{1,0:T(8,128)(2,1)S(1)}, bf16[384,384]{1,0:T(8,128)(2,1)S(1)}, u32[]{:S(2)}, u32[]{:S(2)}) %collective-permute-start.16) | collective-permute-done | bytes 294944 | tf_op jit(solution)/shard_map/ppermute | solution.py:671
  59.8 5.9 %collective-permute-done.20.refs_2_ = bf16[384,384]{1,0:T(8,128)(2,1)S(1)} collective-permute-done((bf16[384,384]{1,0:T(8,128)(2,1)S(1)}, bf16[384,384]{1,0:T(8,128)(2,1)S(1)}, u32[]{:S(2)}, u32[]{:S(2)}) %collective-permute-start.20) | collective-permute-done | bytes 294944 | tf_op jit(solution)/shard_map/ppermute | solution.py:671
  65.7 4.2 %collective-permute-done.19.near_out = bf16[384,384]{1,0:T(8,128)(2,1)S(1)} collective-permute-done((bf16[384,384]{1,0:T(8,128)(2,1)S(1)}, bf16[384,384]{1,0:T(8,128)(2,1)S(1)}, u32[]{:S(2)}, u32[]{:S(2)}) %collective-permute-start.19) | collective-permute-done | bytes 294944 | tf_op jit(solution)/shard_map/ppermute | solution.py:671
  73.2 5.6 %expert.3 = (bf16[320,768]{1,0:T(8,128)(2,1)S(1)}, bf16[320,768]{1,0:T(8,128)(2,1)S(1)}, bf16[640,1536]{1,0:T(8,128)(2,1)S(1)}, bf16[640,1536]{1,0:T(8,128)(2,1)S(1)}) custom-call(bf16[320,768]{1,0:T(8,128)(2,1)S(1)} %collective-permute-done.18.refs_0_.refs_2_, bf16[320,768]{1,0:T(8,128)(2,1)S(1)} %collective-permute-done.25.refs_1_.refs_3_, ...), custom_call_target="tpu_custom_call" | custom-call | flops 3019898880 | bytes 1024 | tf_op jit(solution)/shard_map/expert/pallas_call | solution.py:40
  78.8 5.5 %expert.2 = (bf16[320,768]{1,0:T(8,128)(2,1)S(1)}, bf16[320,768]{1,0:T(8,128)(2,1)S(1)}, bf16[640,1536]{1,0:T(8,128)(2,1)S(1)}, bf16[640,1536]{1,0:T(8,128)(2,1)S(1)}) custom-call(bf16[320,768]{1,0:T(8,128)(2,1)S(1)} %get-tuple-element.190.refs_0_, bf16[320,768]{1,0:T(8,128)(2,1)S(1)} %collective-permute-done.17.refs_1_, ...), custom_call_target="tpu_custom_call" | custom-call | flops 3019898880 | bytes 1024 | tf_op jit(solution)/shard_map/expert/pallas_call | solution.py:40
  84.4 4.0 %expert_grad.1 = (bf16[1536,384]{1,0:T(8,128)(2,1)S(1)}, bf16[1536,384]{1,0:T(8,128)(2,1)S(1)}) custom-call(bf16[320,768]{1,0:T(8,128)(2,1)S(1)} %get-tuple-element.190.refs_0_, bf16[320,768]{1,0:T(8,128)(2,1)S(1)} %collective-permute-done.17.refs_1_, bf16[320,768]{1,0:T(8,128)(2,1)S(1)} %collective-permute-done.18.refs_0_.refs_2_, ...), custom_call_target="tpu_custom_call" | custom-call | flops 3019898880 | bytes 1024 | tf_op jit(solution)/shard_map/expert_grad/pallas_call | solution.py:40
  88.6 1.4 collective-permute-start.27
  90.0 2.1 %collective-permute-start.28 = (bf16[320,768]{1,0:T(8,128)(2,1)S(1)}, bf16[320,768]{1,0:T(8,128)(2,1)S(1)}, u32[]{:S(2)}, u32[]{:S(2)}) collective-permute-start(bf16[320,768]{1,0:T(8,128)(2,1)S(1)} %get-tuple-element.220), channel_id=1, source_target_pairs={{0,8},{1,9},{2,10},{3,11},{4,12},{5,13},{6,14},{7,15},{8,0},{9,1},... | collective-permute-start | bytes 1474568 | tf_op jit(solution)/shard_map/ppermute | solution.py:671
  92.1 1.0 split.1
  93.1 1.5 collective-permute-start.30
  95.2 17.4 %collective-permute-done.27.refs_1_ = bf16[320,768]{1,0:T(8,128)(2,1)S(1)} collective-permute-done((bf16[320,768]{1,0:T(8,128)(2,1)S(1)}, bf16[320,768]{1,0:T(8,128)(2,1)S(1)}, u32[]{:S(2)}, u32[]{:S(2)}) %collective-permute-start.27) | collective-permute-done | bytes 491552 | tf_op jit(solution)/shard_map/ppermute | solution.py:671
  112.8 1.1 collective-permute-done.28.refs_2_
  115.1 1.4 collective-permute-start.40
  117.1 1.9 %collective-permute-start.45 = (bf16[768,384]{1,0:T(8,128)(2,1)S(1)}, bf16[768,384]{1,0:T(8,128)(2,1)S(1)}, u32[]{:S(2)}, u32[]{:S(2)}) collective-permute-start(bf16[768,384]{1,0:T(8,128)(2,1)S(1)} %away.1), channel_id=1, source_target_pairs={{0,16},{1,17},{2,18},{3,19},{4,20},{5,21},{6,22},{7,23},{8,24},{9,... | collective-permute-start | bytes 1769480 | tf_op jit(solution)/shard_map/ppermute | solution.py:671
  119.0 5.1 %combine.1 = (bf16[512,384]{1,0:T(8,128)(2,1)}, f32[512,384]{1,0:T(8,128)S(1)}, bf16[512,384]{1,0:T(8,128)(2,1)S(1)}, bf16[384,512]{1,0:T(8,128)(2,1)S(1)}) custom-call(f32[512,384]{1,0:T(8,128)S(1)} %get-tuple-element.173.middle, bf16[512,384]{1,0:T(8,128)(2,1)S(1)} %get-tuple-element.174.normed_two, f32[512,128]{1,0:T(8,128)S(1)} %get-tuple-element.175.probs, ...), custom_call_target="tpu_custom_call" | custom-call | flops 1509949440 | bytes 1024 | tf_op jit(solution)/shard_map/combine/pallas_call | solution.py:40
  124.1 9.5 %backward.1 = (bf16[512,384]{1,0:T(8,128)(2,1)S(1)}, bf16[256,768]{1,0:T(8,128)(2,1)S(1)}, bf16[256,768]{1,0:T(8,128)(2,1)S(1)}, f32[512,768]{1,0:T(8,128)S(1)},...) custom-call(bf16[1024,1152]{1,0:T(8,128)(2,1)S(1)} %get-tuple-elemen, ...), custom_call_target="tpu_custom_call" | custom-call | bytes 1024 | tf_op jit(solution)/shard_map/backward/pallas_call | solution.py:40
  136.4 0.8 collective-permute-start.43
  137.3 2.2 %collective-permute-start.44 = (bf16[48,1664]{1,0:T(8,128)(2,1)S(1)}, bf16[48,1664]{1,0:T(8,128)(2,1)S(1)}, u32[]{:S(2)}, u32[]{:S(2)}) collective-permute-start(bf16[48,1664]{1,0:T(8,128)(2,1)S(1)} %get-tuple-element.252), channel_id=1, source_target_pairs={{0,6},{1,7},{2,4},{3,5},{4,2},{5,3},{6,0},{7,1},{8,14},{9,15},{10,... | collective-permute-start | bytes 479240 | tf_op jit(solution)/shard_map/ppermute | solution.py:671
  139.4 3.4 %collective-permute-done.42.refs_0_ = bf16[48,1664]{1,0:T(8,128)(2,1)S(1)} collective-permute-done((bf16[48,1664]{1,0:T(8,128)(2,1)S(1)}, bf16[48,1664]{1,0:T(8,128)(2,1)S(1)}, u32[]{:S(2)}, u32[]{:S(2)}) %collective-permute-start.42) | collective-permute-done | bytes 159776 | tf_op jit(solution)/shard_map/ppermute | solution.py:671
  143.1 2.8 %collective-permute-done.44.refs_2_ = bf16[48,1664]{1,0:T(8,128)(2,1)S(1)} collective-permute-done((bf16[48,1664]{1,0:T(8,128)(2,1)S(1)}, bf16[48,1664]{1,0:T(8,128)(2,1)S(1)}, u32[]{:S(2)}, u32[]{:S(2)}) %collective-permute-start.44) | collective-permute-done | bytes 159776 | tf_op jit(solution)/shard_map/ppermute | solution.py:671
  145.9 1.6 collective-permute-start.47
  147.5 1.3 collective-permute-start.48
  148.9 7.0 %collective-permute-start.46 = (bf16[12,1664]{1,0:T(8,128)(2,1)S(1)}, bf16[12,1664]{1,0:T(8,128)(2,1)S(1)}, u32[]{:S(2)}, u32[]{:S(2)}) collective-permute-start(bf16[12,1664]{1,0:T(8,128)(2,1)S(1)} %get-tuple-element.259), channel_id=1, source_target_pairs={{0,8},{1,9},{2,10},{3,11},{4,12},{5,13},{6,14},{7,15},{8,0},{9,1},... | collective-permute-start | bytes 119816 | tf_op jit(solution)/shard_map/ppermute | solution.py:671
  156.2 2.1 %collective-permute-start.50 = (bf16[12,1664]{1,0:T(8,128)(2,1)S(1)}, bf16[12,1664]{1,0:T(8,128)(2,1)S(1)}, u32[]{:S(2)}, u32[]{:S(2)}) collective-permute-start(bf16[12,1664]{1,0:T(8,128)(2,1)S(1)} %get-tuple-element.271), channel_id=1, source_target_pairs={{0,24},{1,25},{2,26},{3,27},{4,28},{5,29},{6,30},{7,31},{8,16},{9,... | collective-permute-start | bytes 119816 | tf_op jit(solution)/shard_map/ppermute | solution.py:671
  158.3 2.4 %finish.1 = bf16[512,384]{1,0:T(8,128)(2,1)} custom-call(bf16[512,384]{1,0:T(8,128)(2,1)S(1)} %get-tuple-element.260.dq, f32[512,768]{1,0:T(8,128)S(1)} %get-tuple-element.261.inner, bf16[256,768]{1,0:T(8,128)(2,1)S(1)} %collective-permute-done.47.from_low, bf16[256,768]{1,0:T(8,128)(2,1)S(1)} %collective-permute-done.48.from_high, ...), custom_call_target="tpu_custom_call" | custom-call | flops 754974720 | bytes 1024 | tf_op jit(solution)/shard_map/finish/pallas_call | solution.py:40
  160.7 2.2 %collective-permute-done.46.refs_0_ = bf16[12,1664]{1,0:T(8,128)(2,1)S(1)} collective-permute-done((bf16[12,1664]{1,0:T(8,128)(2,1)S(1)}, bf16[12,1664]{1,0:T(8,128)(2,1)S(1)}, u32[]{:S(2)}, u32[]{:S(2)}) %collective-permute-start.46) | collective-permute-done | bytes 39968 | tf_op jit(solution)/shard_map/ppermute | solution.py:671
  162.9 1.5 collective-permute-done.49.refs_1_
  164.4 1.3 final.1
  (92 shorter events, 14.4 us)
Async XLA Ops:
  2.1 18.0 %collective-permute-start.2 = (bf16[256,512]{1,0:T(8,128)(2,1)S(1)}, bf16[256,512]{1,0:T(8,128)(2,1)S(1)}, u32[]{:S(2)}, u32[]{:S(2)}) collective-permute-start(bf16[256,512]{1,0:T(8,128)(2,1)S(1)} %get-tuple-element.153), channel_id=1, source_target_pairs={{0,1},{1,2},{2,3},{3,4},{4,5},{5,6},{6,7},{7,8},{8,9},{9,10},{10,1... | collective-permute-start | bytes 786440 | tf_op jit(solution)/shard_map/ppermute | solution.py:743
  4.5 15.6 %collective-permute-start.3 = (bf16[256,512]{1,0:T(8,128)(2,1)S(1)}, bf16[256,512]{1,0:T(8,128)(2,1)S(1)}, u32[]{:S(2)}, u32[]{:S(2)}) collective-permute-start(bf16[256,512]{1,0:T(8,128)(2,1)S(1)} %get-tuple-element.154), channel_id=1, source_target_pairs={{1,0},{2,1},{3,2},{4,3},{5,4},{6,5},{7,6},{8,7},{9,8},{10,9},{11,1... | collective-permute-start | bytes 786440 | tf_op jit(solution)/shard_map/ppermute | solution.py:744
  5.8 14.3 %collective-permute-start = (bf16[12,1664]{1,0:T(8,128)(2,1)S(1)}, bf16[12,1664]{1,0:T(8,128)(2,1)S(1)}, u32[]{:S(2)}, u32[]{:S(2)}) collective-permute-start(bf16[12,1664]{1,0:T(8,128)(2,1)S(1)} %get-tuple-element.149.refs_0_), channel_id=1, source_target_pairs={{0,24},{1,25},{2,26},{3,27},{4,28},{5,29},{6,30},{7,31},{8,16},{9,... | collective-permute-start | bytes 119816 | tf_op jit(solution)/shard_map/ppermute | solution.py:671
  14.6 5.5 %collective-permute-start.1 = (bf16[12,1664]{1,0:T(8,128)(2,1)S(1)}, bf16[12,1664]{1,0:T(8,128)(2,1)S(1)}, u32[]{:S(2)}, u32[]{:S(2)}) collective-permute-start(bf16[12,1664]{1,0:T(8,128)(2,1)S(1)} %get-tuple-element.149.refs_0_), channel_id=1, source_target_pairs={{0,8},{1,9},{2,10},{3,11},{4,12},{5,13},{6,14},{7,15},{8,0},{9,1},... | collective-permute-start | bytes 119816 | tf_op jit(solution)/shard_map/ppermute | solution.py:671
  14.6 6.7 %collective-permute-start.4 = (bf16[12,1664]{1,0:T(8,128)(2,1)S(1)}, bf16[12,1664]{1,0:T(8,128)(2,1)S(1)}, u32[]{:S(2)}, u32[]{:S(2)}) collective-permute-start(bf16[12,1664]{1,0:T(8,128)(2,1)S(1)} %get-tuple-element.149.refs_0_), channel_id=1, source_target_pairs={{0,16},{1,17},{2,18},{3,19},{4,20},{5,21},{6,22},{7,23},{8,24},{9,... | collective-permute-start | bytes 119816 | tf_op jit(solution)/shard_map/ppermute | solution.py:671
  21.3 6.3 %collective-permute-start.7 = (bf16[48,1664]{1,0:T(8,128)(2,1)S(1)}, bf16[48,1664]{1,0:T(8,128)(2,1)S(1)}, u32[]{:S(2)}, u32[]{:S(2)}) collective-permute-start(bf16[48,1664]{1,0:T(8,128)(2,1)S(1)} %join.2.refs_0_), channel_id=1, source_target_pairs={{0,6},{1,7},{2,4},{3,5},{4,2},{5,3},{6,0},{7,1},{8,14},{9,15},{10,... | collective-permute-start | bytes 479240 | tf_op jit(solution)/shard_map/ppermute | solution.py:671
  21.4 7.1 %collective-permute-start.6 = (bf16[48,1664]{1,0:T(8,128)(2,1)S(1)}, bf16[48,1664]{1,0:T(8,128)(2,1)S(1)}, u32[]{:S(2)}, u32[]{:S(2)}) collective-permute-start(bf16[48,1664]{1,0:T(8,128)(2,1)S(1)} %join.2.refs_0_), channel_id=1, source_target_pairs={{0,4},{1,5},{2,6},{3,7},{4,0},{5,1},{6,2},{7,3},{8,12},{9,13},{10,... | collective-permute-start | bytes 479240 | tf_op jit(solution)/shard_map/ppermute | solution.py:671
  21.5 7.0 %collective-permute-start.5 = (bf16[48,1664]{1,0:T(8,128)(2,1)S(1)}, bf16[48,1664]{1,0:T(8,128)(2,1)S(1)}, u32[]{:S(2)}, u32[]{:S(2)}) collective-permute-start(bf16[48,1664]{1,0:T(8,128)(2,1)S(1)} %join.2.refs_0_), channel_id=1, source_target_pairs={{0,2},{1,3},{2,0},{3,1},{4,6},{5,7},{6,4},{7,5},{8,10},{9,11},{10,... | collective-permute-start | bytes 479240 | tf_op jit(solution)/shard_map/ppermute | solution.py:671
  24.9 24.4 %collective-permute-start.10 = (bf16[768,384]{1,0:T(8,128)(2,1)S(1)}, bf16[768,384]{1,0:T(8,128)(2,1)S(1)}, u32[]{:S(2)}, u32[]{:S(2)}) collective-permute-start(bf16[768,384]{1,0:T(8,128)(2,1)S(1)} %quarter.1.near_one), channel_id=1, source_target_pairs={{0,16},{1,17},{2,18},{3,19},{4,20},{5,21},{6,22},{7,23},{8,24},{9,... | collective-permute-start | bytes 1769480 | tf_op jit(solution)/shard_map/ppermute | solution.py:671
  28.5 3.4 %collective-permute-start.8 = (bf16[96,1664]{1,0:T(8,128)(2,1)S(1)}, bf16[96,1664]{1,0:T(8,128)(2,1)S(1)}, u32[]{:S(2)}, u32[]{:S(2)}) collective-permute-start(bf16[96,1664]{1,0:T(8,128)(2,1)S(1)} %get-tuple-element.171.near_one), channel_id=1, source_target_pairs={{0,1},{1,0},{2,3},{3,2},{4,5},{5,4},{6,7},{7,6},{8,9},{9,8},{10,11... | collective-permute-start | bytes 958472 | tf_op jit(solution)/shard_map/ppermute | solution.py:671
  28.6 3.3 %collective-permute-start.9 = (bf16[96,1664]{1,0:T(8,128)(2,1)S(1)}, bf16[96,1664]{1,0:T(8,128)(2,1)S(1)}, u32[]{:S(2)}, u32[]{:S(2)}) collective-permute-start(bf16[96,1664]{1,0:T(8,128)(2,1)S(1)} %get-tuple-element.172.near_two), channel_id=1, source_target_pairs={{0,1},{1,0},{2,3},{3,2},{4,5},{5,4},{6,7},{7,6},{8,9},{9,8},{10,11... | collective-permute-start | bytes 958472 | tf_op jit(solution)/shard_map/ppermute | solution.py:671
  29.1 10.4 %collective-permute-start.11 = (bf16[384,384]{1,0:T(8,128)(2,1)S(1)}, bf16[384,384]{1,0:T(8,128)(2,1)S(1)}, u32[]{:S(2)}, u32[]{:S(2)}) collective-permute-start(bf16[384,384]{1,0:T(8,128)(2,1)S(1)} %bitcast.15), channel_id=1, source_target_pairs={{0,2},{1,3},{2,0},{3,1},{4,6},{5,7},{6,4},{7,5},{8,10},{9,11},{10,... | collective-permute-start | bytes 884744 | tf_op jit(solution)/shard_map/ppermute | solution.py:671
  39.5 1.6 collective-permute-start.12
  39.5 1.9 %collective-permute-start.13 = (bf16[160,768]{1,0:T(8,128)(2,1)S(1)}, bf16[160,768]{1,0:T(8,128)(2,1)S(1)}, u32[]{:S(2)}, u32[]{:S(2)}) collective-permute-start(bf16[160,768]{1,0:T(8,128)(2,1)S(1)} %get-tuple-element.186), channel_id=1, source_target_pairs={{0,1},{1,0},{2,3},{3,2},{4,5},{5,4},{6,7},{7,6},{8,9},{9,8},{10,11... | collective-permute-start | bytes 737288 | tf_op jit(solution)/shard_map/ppermute | solution.py:671
  40.0 1.7 %collective-permute-start.14 = (bf16[160,768]{1,0:T(8,128)(2,1)S(1)}, bf16[160,768]{1,0:T(8,128)(2,1)S(1)}, u32[]{:S(2)}, u32[]{:S(2)}) collective-permute-start(bf16[160,768]{1,0:T(8,128)(2,1)S(1)} %get-tuple-element.187), channel_id=1, source_target_pairs={{0,1},{1,0},{2,3},{3,2},{4,5},{5,4},{6,7},{7,6},{8,9},{9,8},{10,11... | collective-permute-start | bytes 737288 | tf_op jit(solution)/shard_map/ppermute | solution.py:671
  40.1 2.0 %collective-permute-start.15 = (bf16[160,768]{1,0:T(8,128)(2,1)S(1)}, bf16[160,768]{1,0:T(8,128)(2,1)S(1)}, u32[]{:S(2)}, u32[]{:S(2)}) collective-permute-start(bf16[160,768]{1,0:T(8,128)(2,1)S(1)} %get-tuple-element.188), channel_id=1, source_target_pairs={{0,1},{1,0},{2,3},{3,2},{4,5},{5,4},{6,7},{7,6},{8,9},{9,8},{10,11... | collective-permute-start | bytes 737288 | tf_op jit(solution)/shard_map/ppermute | solution.py:671
  42.2 17.6 %collective-permute-start.17 = (bf16[320,768]{1,0:T(8,128)(2,1)S(1)}, bf16[320,768]{1,0:T(8,128)(2,1)S(1)}, u32[]{:S(2)}, u32[]{:S(2)}) collective-permute-start(bf16[320,768]{1,0:T(8,128)(2,1)S(1)} %get-tuple-element.193), channel_id=1, source_target_pairs={{0,4},{1,5},{2,6},{3,7},{4,0},{5,1},{6,2},{7,3},{8,12},{9,13},{10,... | collective-permute-start | bytes 1474568 | tf_op jit(solution)/shard_map/ppermute | solution.py:671
  43.0 16.8 %collective-permute-start.18 = (bf16[320,768]{1,0:T(8,128)(2,1)S(1)}, bf16[320,768]{1,0:T(8,128)(2,1)S(1)}, u32[]{:S(2)}, u32[]{:S(2)}) collective-permute-start(bf16[320,768]{1,0:T(8,128)(2,1)S(1)} %get-tuple-element.194), channel_id=1, source_target_pairs={{0,8},{1,9},{2,10},{3,11},{4,12},{5,13},{6,14},{7,15},{8,0},{9,1},... | collective-permute-start | bytes 1474568 | tf_op jit(solution)/shard_map/ppermute | solution.py:671
  49.4 10.0 %collective-permute-start.16 = (bf16[384,384]{1,0:T(8,128)(2,1)S(1)}, bf16[384,384]{1,0:T(8,128)(2,1)S(1)}, u32[]{:S(2)}, u32[]{:S(2)}) collective-permute-start(bf16[384,384]{1,0:T(8,128)(2,1)S(1)} %get-tuple-element.192.refs_1_), channel_id=1, source_target_pairs={{0,2},{1,3},{2,0},{3,1},{4,6},{5,7},{6,4},{7,5},{8,10},{9,11},{10,... | collective-permute-start | bytes 884744 | tf_op jit(solution)/shard_map/ppermute | solution.py:671
  50.8 14.9 %collective-permute-start.20 = (bf16[384,384]{1,0:T(8,128)(2,1)S(1)}, bf16[384,384]{1,0:T(8,128)(2,1)S(1)}, u32[]{:S(2)}, u32[]{:S(2)}) collective-permute-start(bf16[384,384]{1,0:T(8,128)(2,1)S(1)} %get-tuple-element.198.refs_0_), channel_id=1, source_target_pairs={{0,2},{1,3},{2,0},{3,1},{4,6},{5,7},{6,4},{7,5},{8,10},{9,11},{10,... | collective-permute-start | bytes 884744 | tf_op jit(solution)/shard_map/ppermute | solution.py:671
  51.5 18.5 %collective-permute-start.19 = (bf16[384,384]{1,0:T(8,128)(2,1)S(1)}, bf16[384,384]{1,0:T(8,128)(2,1)S(1)}, u32[]{:S(2)}, u32[]{:S(2)}) collective-permute-start(bf16[384,384]{1,0:T(8,128)(2,1)S(1)} %bitcast.16), channel_id=1, source_target_pairs={{0,2},{1,3},{2,0},{3,1},{4,6},{5,7},{6,4},{7,5},{8,10},{9,11},{10,... | collective-permute-start | bytes 884744 | tf_op jit(solution)/shard_map/ppermute | solution.py:671
  59.4 12.0 %collective-permute-start.25 = (bf16[320,768]{1,0:T(8,128)(2,1)S(1)}, bf16[320,768]{1,0:T(8,128)(2,1)S(1)}, u32[]{:S(2)}, u32[]{:S(2)}) collective-permute-start(bf16[320,768]{1,0:T(8,128)(2,1)S(1)} %get-tuple-element.207), channel_id=1, source_target_pairs={{0,12},{1,13},{2,14},{3,15},{4,8},{5,9},{6,10},{7,11},{8,4},{9,5},... | collective-permute-start | bytes 1474568 | tf_op jit(solution)/shard_map/ppermute | solution.py:671
  70.3 1.6 collective-permute-start.21
  70.4 2.0 %collective-permute-start.22 = (bf16[384,384]{1,0:T(8,128)(2,1)S(1)}, bf16[384,384]{1,0:T(8,128)(2,1)S(1)}, u32[]{:S(2)}, u32[]{:S(2)}) collective-permute-start(bf16[384,384]{1,0:T(8,128)(2,1)S(1)} %get-tuple-element.202), channel_id=1, source_target_pairs={{0,1},{1,0},{2,3},{3,2},{4,5},{5,4},{6,7},{7,6},{8,9},{9,8},{10,11... | collective-permute-start | bytes 884744 | tf_op jit(solution)/shard_map/ppermute | solution.py:671
  70.9 1.9 %collective-permute-start.23 = (bf16[384,384]{1,0:T(8,128)(2,1)S(1)}, bf16[384,384]{1,0:T(8,128)(2,1)S(1)}, u32[]{:S(2)}, u32[]{:S(2)}) collective-permute-start(bf16[384,384]{1,0:T(8,128)(2,1)S(1)} %get-tuple-element.203), channel_id=1, source_target_pairs={{0,1},{1,0},{2,3},{3,2},{4,5},{5,4},{6,7},{7,6},{8,9},{9,8},{10,11... | collective-permute-start | bytes 884744 | tf_op jit(solution)/shard_map/ppermute | solution.py:671
  71.0 2.3 %collective-permute-start.24 = (bf16[384,384]{1,0:T(8,128)(2,1)S(1)}, bf16[384,384]{1,0:T(8,128)(2,1)S(1)}, u32[]{:S(2)}, u32[]{:S(2)}) collective-permute-start(bf16[384,384]{1,0:T(8,128)(2,1)S(1)} %get-tuple-element.204), channel_id=1, source_target_pairs={{0,1},{1,0},{2,3},{3,2},{4,5},{5,4},{6,7},{7,6},{8,9},{9,8},{10,11... | collective-permute-start | bytes 884744 | tf_op jit(solution)/shard_map/ppermute | solution.py:671
  88.4 3.7 %collective-permute-start.26 = (bf16[1536,384]{1,0:T(8,128)(2,1)S(1)}, bf16[1536,384]{1,0:T(8,128)(2,1)S(1)}, u32[]{:S(2)}, u32[]{:S(2)}) collective-permute-start(bf16[1536,384]{1,0:T(8,128)(2,1)S(1)} %get-tuple-element.213), channel_id=1, source_target_pairs={{0,1},{1,0},{2,3},{3,2},{4,5},{5,4},{6,7},{7,6},{8,9},{9,8},{10,11... | collective-permute-start | bytes 3538952 | tf_op jit(solution)/shard_map/ppermute | solution.py:671
  88.6 24.0 %collective-permute-start.27 = (bf16[320,768]{1,0:T(8,128)(2,1)S(1)}, bf16[320,768]{1,0:T(8,128)(2,1)S(1)}, u32[]{:S(2)}, u32[]{:S(2)}) collective-permute-start(bf16[320,768]{1,0:T(8,128)(2,1)S(1)} %get-tuple-element.218), channel_id=1, source_target_pairs={{0,4},{1,5},{2,6},{3,7},{4,0},{5,1},{6,2},{7,3},{8,12},{9,13},{10,... | collective-permute-start | bytes 1474568 | tf_op jit(solution)/shard_map/ppermute | solution.py:671
  90.0 22.8 %collective-permute-start.29 = (bf16[320,768]{1,0:T(8,128)(2,1)S(1)}, bf16[320,768]{1,0:T(8,128)(2,1)S(1)}, u32[]{:S(2)}, u32[]{:S(2)}) collective-permute-start(bf16[320,768]{1,0:T(8,128)(2,1)S(1)} %get-tuple-element.221), channel_id=1, source_target_pairs={{0,12},{1,13},{2,14},{3,15},{4,8},{5,9},{6,10},{7,11},{8,4},{9,5},... | collective-permute-start | bytes 1474568 | tf_op jit(solution)/shard_map/ppermute | solution.py:671
  90.0 23.9 %collective-permute-start.28 = (bf16[320,768]{1,0:T(8,128)(2,1)S(1)}, bf16[320,768]{1,0:T(8,128)(2,1)S(1)}, u32[]{:S(2)}, u32[]{:S(2)}) collective-permute-start(bf16[320,768]{1,0:T(8,128)(2,1)S(1)} %get-tuple-element.220), channel_id=1, source_target_pairs={{0,8},{1,9},{2,10},{3,11},{4,12},{5,13},{6,14},{7,15},{8,0},{9,1},... | collective-permute-start | bytes 1474568 | tf_op jit(solution)/shard_map/ppermute | solution.py:671
  93.1 19.5 %collective-permute-start.30 = (bf16[384,384]{1,0:T(8,128)(2,1)S(1)}, bf16[384,384]{1,0:T(8,128)(2,1)S(1)}, u32[]{:S(2)}, u32[]{:S(2)}) collective-permute-start(bf16[384,384]{1,0:T(8,128)(2,1)S(1)} %get-tuple-element.223), channel_id=1, source_target_pairs={{0,2},{1,3},{2,0},{3,1},{4,6},{5,7},{6,4},{7,5},{8,10},{9,11},{10,... | collective-permute-start | bytes 884744 | tf_op jit(solution)/shard_map/ppermute | solution.py:671
  94.6 18.0 %collective-permute-start.31 = (bf16[384,384]{1,0:T(8,128)(2,1)S(1)}, bf16[384,384]{1,0:T(8,128)(2,1)S(1)}, u32[]{:S(2)}, u32[]{:S(2)}) collective-permute-start(bf16[384,384]{1,0:T(8,128)(2,1)S(1)} %get-tuple-element.224), channel_id=1, source_target_pairs={{0,2},{1,3},{2,0},{3,1},{4,6},{5,7},{6,4},{7,5},{8,10},{9,11},{10,... | collective-permute-start | bytes 884744 | tf_op jit(solution)/shard_map/ppermute | solution.py:671
  114.0 2.5 %collective-permute-start.32 = (bf16[160,768]{1,0:T(8,128)(2,1)S(1)}, bf16[160,768]{1,0:T(8,128)(2,1)S(1)}, u32[]{:S(2)}, u32[]{:S(2)}) collective-permute-start(bf16[160,768]{1,0:T(8,128)(2,1)S(1)} %get-tuple-element.227), channel_id=1, source_target_pairs={{0,1},{1,0},{2,3},{3,2},{4,5},{5,4},{6,7},{7,6},{8,9},{9,8},{10,11... | collective-permute-start | bytes 737288 | tf_op jit(solution)/shard_map/ppermute | solution.py:671
  114.1 3.0 %collective-permute-start.33 = (bf16[160,768]{1,0:T(8,128)(2,1)S(1)}, bf16[160,768]{1,0:T(8,128)(2,1)S(1)}, u32[]{:S(2)}, u32[]{:S(2)}) collective-permute-start(bf16[160,768]{1,0:T(8,128)(2,1)S(1)} %get-tuple-element.228), channel_id=1, source_target_pairs={{0,1},{1,0},{2,3},{3,2},{4,5},{5,4},{6,7},{7,6},{8,9},{9,8},{10,11... | collective-permute-start | bytes 737288 | tf_op jit(solution)/shard_map/ppermute | solution.py:671
  114.5 4.4 %collective-permute-start.34 = (bf16[160,768]{1,0:T(8,128)(2,1)S(1)}, bf16[160,768]{1,0:T(8,128)(2,1)S(1)}, u32[]{:S(2)}, u32[]{:S(2)}) collective-permute-start(bf16[160,768]{1,0:T(8,128)(2,1)S(1)} %get-tuple-element.229), channel_id=1, source_target_pairs={{0,1},{1,0},{2,3},{3,2},{4,5},{5,4},{6,7},{7,6},{8,9},{9,8},{10,11... | collective-permute-start | bytes 737288 | tf_op jit(solution)/shard_map/ppermute | solution.py:671
  114.6 4.3 %collective-permute-start.35 = (bf16[160,768]{1,0:T(8,128)(2,1)S(1)}, bf16[160,768]{1,0:T(8,128)(2,1)S(1)}, u32[]{:S(2)}, u32[]{:S(2)}) collective-permute-start(bf16[160,768]{1,0:T(8,128)(2,1)S(1)} %get-tuple-element.230), channel_id=1, source_target_pairs={{0,1},{1,0},{2,3},{3,2},{4,5},{5,4},{6,7},{7,6},{8,9},{9,8},{10,11... | collective-permute-start | bytes 737288 | tf_op jit(solution)/shard_map/ppermute | solution.py:671
  115.1 19.1 %collective-permute-start.40 = (bf16[384,384]{1,0:T(8,128)(2,1)S(1)}, bf16[384,384]{1,0:T(8,128)(2,1)S(1)}, u32[]{:S(2)}, u32[]{:S(2)}) collective-permute-start(bf16[384,384]{1,0:T(8,128)(2,1)S(1)} %get-tuple-element.243), channel_id=1, source_target_pairs={{0,2},{1,3},{2,0},{3,1},{4,6},{5,7},{6,4},{7,5},{8,10},{9,11},{10,... | collective-permute-start | bytes 884744 | tf_op jit(solution)/shard_map/ppermute | solution.py:671
  116.5 17.8 %collective-permute-start.41 = (bf16[384,384]{1,0:T(8,128)(2,1)S(1)}, bf16[384,384]{1,0:T(8,128)(2,1)S(1)}, u32[]{:S(2)}, u32[]{:S(2)}) collective-permute-start(bf16[384,384]{1,0:T(8,128)(2,1)S(1)} %get-tuple-element.244), channel_id=1, source_target_pairs={{0,2},{1,3},{2,0},{3,1},{4,6},{5,7},{6,4},{7,5},{8,10},{9,11},{10,... | collective-permute-start | bytes 884744 | tf_op jit(solution)/shard_map/ppermute | solution.py:671
  117.1 28.8 %collective-permute-start.45 = (bf16[768,384]{1,0:T(8,128)(2,1)S(1)}, bf16[768,384]{1,0:T(8,128)(2,1)S(1)}, u32[]{:S(2)}, u32[]{:S(2)}) collective-permute-start(bf16[768,384]{1,0:T(8,128)(2,1)S(1)} %away.1), channel_id=1, source_target_pairs={{0,16},{1,17},{2,18},{3,19},{4,20},{5,21},{6,22},{7,23},{8,24},{9,... | collective-permute-start | bytes 1769480 | tf_op jit(solution)/shard_map/ppermute | solution.py:671
  133.6 1.6 collective-permute-start.37
  135.9 7.0 %collective-permute-start.42 = (bf16[48,1664]{1,0:T(8,128)(2,1)S(1)}, bf16[48,1664]{1,0:T(8,128)(2,1)S(1)}, u32[]{:S(2)}, u32[]{:S(2)}) collective-permute-start(bf16[48,1664]{1,0:T(8,128)(2,1)S(1)} %get-tuple-element.250), channel_id=1, source_target_pairs={{0,2},{1,3},{2,0},{3,1},{4,6},{5,7},{6,4},{7,5},{8,10},{9,11},{10,... | collective-permute-start | bytes 479240 | tf_op jit(solution)/shard_map/ppermute | solution.py:671
  136.4 6.7 %collective-permute-start.43 = (bf16[48,1664]{1,0:T(8,128)(2,1)S(1)}, bf16[48,1664]{1,0:T(8,128)(2,1)S(1)}, u32[]{:S(2)}, u32[]{:S(2)}) collective-permute-start(bf16[48,1664]{1,0:T(8,128)(2,1)S(1)} %get-tuple-element.251), channel_id=1, source_target_pairs={{0,4},{1,5},{2,6},{3,7},{4,0},{5,1},{6,2},{7,3},{8,12},{9,13},{10,... | collective-permute-start | bytes 479240 | tf_op jit(solution)/shard_map/ppermute | solution.py:671
  137.3 8.6 %collective-permute-start.44 = (bf16[48,1664]{1,0:T(8,128)(2,1)S(1)}, bf16[48,1664]{1,0:T(8,128)(2,1)S(1)}, u32[]{:S(2)}, u32[]{:S(2)}) collective-permute-start(bf16[48,1664]{1,0:T(8,128)(2,1)S(1)} %get-tuple-element.252), channel_id=1, source_target_pairs={{0,6},{1,7},{2,4},{3,5},{4,2},{5,3},{6,0},{7,1},{8,14},{9,15},{10,... | collective-permute-start | bytes 479240 | tf_op jit(solution)/shard_map/ppermute | solution.py:671
  145.9 12.4 %collective-permute-start.47 = (bf16[256,768]{1,0:T(8,128)(2,1)S(1)}, bf16[256,768]{1,0:T(8,128)(2,1)S(1)}, u32[]{:S(2)}, u32[]{:S(2)}) collective-permute-start(bf16[256,768]{1,0:T(8,128)(2,1)S(1)} %get-tuple-element.262), channel_id=1, source_target_pairs={{0,1},{1,2},{2,3},{3,4},{4,5},{5,6},{6,7},{7,8},{8,9},{9,10},{10,1... | collective-permute-start | bytes 1179656 | tf_op jit(solution)/shard_map/ppermute | solution.py:967
  147.5 10.8 %collective-permute-start.48 = (bf16[256,768]{1,0:T(8,128)(2,1)S(1)}, bf16[256,768]{1,0:T(8,128)(2,1)S(1)}, u32[]{:S(2)}, u32[]{:S(2)}) collective-permute-start(bf16[256,768]{1,0:T(8,128)(2,1)S(1)} %get-tuple-element.263), channel_id=1, source_target_pairs={{1,0},{2,1},{3,2},{4,3},{5,4},{6,5},{7,6},{8,7},{9,8},{10,9},{11,1... | collective-permute-start | bytes 1179656 | tf_op jit(solution)/shard_map/ppermute | solution.py:966
  148.9 14.0 %collective-permute-start.46 = (bf16[12,1664]{1,0:T(8,128)(2,1)S(1)}, bf16[12,1664]{1,0:T(8,128)(2,1)S(1)}, u32[]{:S(2)}, u32[]{:S(2)}) collective-permute-start(bf16[12,1664]{1,0:T(8,128)(2,1)S(1)} %get-tuple-element.259), channel_id=1, source_target_pairs={{0,8},{1,9},{2,10},{3,11},{4,12},{5,13},{6,14},{7,15},{8,0},{9,1},... | collective-permute-start | bytes 119816 | tf_op jit(solution)/shard_map/ppermute | solution.py:671
  155.9 8.6 %collective-permute-start.49 = (bf16[12,1664]{1,0:T(8,128)(2,1)S(1)}, bf16[12,1664]{1,0:T(8,128)(2,1)S(1)}, u32[]{:S(2)}, u32[]{:S(2)}) collective-permute-start(bf16[12,1664]{1,0:T(8,128)(2,1)S(1)} %get-tuple-element.270), channel_id=1, source_target_pairs={{0,16},{1,17},{2,18},{3,19},{4,20},{5,21},{6,22},{7,23},{8,24},{9,... | collective-permute-start | bytes 119816 | tf_op jit(solution)/shard_map/ppermute | solution.py:671
  156.2 8.2 %collective-permute-start.50 = (bf16[12,1664]{1,0:T(8,128)(2,1)S(1)}, bf16[12,1664]{1,0:T(8,128)(2,1)S(1)}, u32[]{:S(2)}, u32[]{:S(2)}) collective-permute-start(bf16[12,1664]{1,0:T(8,128)(2,1)S(1)} %get-tuple-element.271), channel_id=1, source_target_pairs={{0,24},{1,25},{2,26},{3,27},{4,28},{5,29},{6,30},{7,31},{8,16},{9,... | collective-permute-start | bytes 119816 | tf_op jit(solution)/shard_map/ppermute | solution.py:671
  (11 other events, 119.7 us)

commit v2 on v0

--- a/solution.py
+++ b/solution.py
@@ -13,6 +13,7 @@
 EPSILON = 1e-06
 MASKED = -1e30
 HALO = 256
+RIM = 208
 BLOCK = 128
 WINDOW = BLOCK + 2 * HALO
 LANES = 128
@@ -97,8 +98,8 @@
         own[index * BLOCK : (index + 1) * BLOCK, width:] = jnp.where(
             lane_iota(BLOCK) == 0, upper, lower
         ).astype(BF)
-    low[...] = own[rows - HALO :, :]
-    high[...] = own[:HALO, :]
+    low[...] = own[rows - RIM :, :]
+    high[...] = own[:RIM, :]
 
 
 def quarter_body(width, w_in, w_out, quarter, sems):
@@ -140,15 +141,21 @@
     sel = (lax.broadcasted_iota(jnp.int32, (width, width), 0) == target).astype(F32).astype(BF)
     select[...] = sel
     start = 0
+    blank = jnp.zeros((HALO - RIM, width + LANES), BF)
     for ref in (low, own, high):
-        rows = ref.shape[0]
-        values = dot(ref[:, :width], sel)
+        part = ref[...]
+        if ref is low:
+            part = jnp.concatenate([blank, part], axis=0)
+        if ref is high:
+            part = jnp.concatenate([part, blank], axis=0)
+        rows = part.shape[0]
+        values = dot(part[:, :width], sel)
         mean = jnp.mean(values, axis=1, keepdims=True)
         centered = values - mean
         rstd = lax.rsqrt(jnp.mean(centered * centered, axis=1, keepdims=True) + EPSILON)
         xhat[start : start + rows, :] = centered * rstd
         rstd_out[start : start + rows, :] = jnp.broadcast_to(rstd, (rows, LANES))
-        marks = ref[:, width : width + LANES].astype(F32)
+        marks = part[:, width:].astype(F32)
         column = marks[:, 0:1] * 256.0 + marks[:, 1:2]
         idcol[start : start + rows, :] = jnp.broadcast_to(column, (rows, LANES))
         turned = marks.T
@@ -561,8 +568,8 @@
         return carry
 
     lax.fori_loop(0, rows // BLOCK, attend, 0, unroll=2)
-    rims_low[...] = acc[:HALO, :].astype(BF)
-    rims_high[...] = acc[HALO + rows :, :].astype(BF)
+    rims_low[...] = acc[HALO - RIM : HALO, :].astype(BF)
+    rims_high[...] = acc[HALO + rows : HALO + rows + RIM, :].astype(BF)
     inner[...] = acc[HALO : HALO + rows, :]
     own = normed[HALO : HALO + rows, :]
     query_part = dot(own, dq[...], 0, 0)
@@ -584,8 +591,8 @@
     rows = dq.shape[0]
     experts_lane = 0
     grad[...] = inner[...]
-    grad[:HALO, :] += from_low[...].astype(F32)
-    grad[rows - HALO :, :] += from_high[...].astype(F32)
+    grad[:RIM, :] += from_low[...].astype(F32)
+    grad[rows - RIM :, :] += from_high[...].astype(F32)
     values = dot(dq[...], weights[:, :width], 1, 1) + dot(
         grad[...].astype(BF), weights[:, width:], 1, 1
     )
@@ -722,8 +729,8 @@
         [
             shape((share, 4 * width + LANES), BF),
             shape((rows, width + LANES), BF),
-            shape((HALO, width + LANES), BF),
-            shape((HALO, width + LANES), BF),
+            shape((RIM, width + LANES), BF),
+            shape((RIM, width + LANES), BF),
         ],
         ins,
         scratch=[pltpu.VMEM(x.shape, x.dtype) for x in ins]
@@ -934,8 +941,8 @@
         functools.partial(backward_body, width),
         [
             shape((rows, width), BF),
-            shape((HALO, 2 * width), BF),
-            shape((HALO, 2 * width), BF),
+            shape((RIM, 2 * width), BF),
+            shape((RIM, 2 * width), BF),
             shape((rows, 2 * width), F32),
             shape((half_rows, 4 * width + LANES), F32),
         ]

time: 165 us -> 165 us (level)
  transfers between devices with their start and end apart: 51 -> 51, of which waited for: 28 -> 29; matrix products, arithmetic and copies ran while one was open for 0% -> 0% of each run, Pallas kernels for 18% -> 18%
where the time goes in v2:
time: 165 us
  waiting for transfers between devices  66.8 us (40%)
  starting transfers between devices  50.2 us (30%)
  Pallas kernels  46.9 us (28%)
    ppermute x47, waiting for transfers between devices, swap(): return lax.ppermute(value, 'dp', [(i, i ^ mask) for i in range(devices)])  66.8 us
    pallas_call x21, Pallas kernels, call(): pl.pallas_call(body, out_shape=tuple(outs), in_specs=[spec] * len(ins), o...  46.9 us
    ppermute x47, starting transfers between devices, swap(): return lax.ppermute(value, 'dp', [(i, i ^ mask) for i in range(devices)])  43.3 us
  transfers between devices with their start and end apart: 51, of which 29 were waited for; matrix products, arithmetic and copies ran while one was open for 0% of the time, Pallas kernels for 18%

profile of v2, /device:TPU:0, one launch (start us, length us, event | category | flops | bytes accessed | tf_op | source)
XLA Modules:
  0.0 165.0 jit_solution(10841083428316251796)
XLA Ops:
  0.7 1.4 pack.1
  2.1 2.4 %collective-permute-start.1 = (bf16[208,512]{1,0:T(8,128)(2,1)S(1)}, bf16[208,512]{1,0:T(8,128)(2,1)S(1)}, u32[]{:S(2)}, u32[]{:S(2)}) collective-permute-start(bf16[208,512]{1,0:T(8,128)(2,1)S(1)} %get-tuple-element.144), channel_id=1, source_target_pairs={{0,1},{1,2},{2,3},{3,4},{4,5},{5,6},{6,7},{7,8},{8,9},{9,10},{10,1... | collective-permute-start | bytes 638984 | tf_op jit(solution)/shard_map/ppermute | solution.py:743
  4.5 1.3 collective-permute-start.2
  5.8 6.8 %collective-permute-start = (bf16[12,1664]{1,0:T(8,128)(2,1)S(1)}, bf16[12,1664]{1,0:T(8,128)(2,1)S(1)}, u32[]{:S(2)}, u32[]{:S(2)}) collective-permute-start(bf16[12,1664]{1,0:T(8,128)(2,1)S(1)} %get-tuple-element.143.refs_0_), channel_id=1, source_target_pairs={{0,8},{1,9},{2,10},{3,11},{4,12},{5,13},{6,14},{7,15},{8,0},{9,1},... | collective-permute-start | bytes 119816 | tf_op jit(solution)/shard_map/ppermute | solution.py:671
  12.6 2.6 %collective-permute-start.3 = (bf16[12,1664]{1,0:T(8,128)(2,1)S(1)}, bf16[12,1664]{1,0:T(8,128)(2,1)S(1)}, u32[]{:S(2)}, u32[]{:S(2)}) collective-permute-start(bf16[12,1664]{1,0:T(8,128)(2,1)S(1)} %get-tuple-element.143.refs_0_), channel_id=1, source_target_pairs={{0,16},{1,17},{2,18},{3,19},{4,20},{5,21},{6,22},{7,23},{8,24},{9,... | collective-permute-start | bytes 119816 | tf_op jit(solution)/shard_map/ppermute | solution.py:671
  15.2 1.1 quarter.1.near_one
  16.3 1.3 collective-permute-done.refs_1_
  17.5 1.5 collective-permute-done.3.refs_2_
  19.0 2.1 %collective-permute-done.4.refs_3_ = bf16[12,1664]{1,0:T(8,128)(2,1)S(1)} collective-permute-done((bf16[12,1664]{1,0:T(8,128)(2,1)S(1)}, bf16[12,1664]{1,0:T(8,128)(2,1)S(1)}, u32[]{:S(2)}, u32[]{:S(2)}) %collective-permute-start.4) | collective-permute-done | bytes 39968 | tf_op jit(solution)/shard_map/ppermute | solution.py:671
  21.2 0.7 collective-permute-start.7
  22.4 2.3 %collective-permute-start.5 = (bf16[48,1664]{1,0:T(8,128)(2,1)S(1)}, bf16[48,1664]{1,0:T(8,128)(2,1)S(1)}, u32[]{:S(2)}, u32[]{:S(2)}) collective-permute-start(bf16[48,1664]{1,0:T(8,128)(2,1)S(1)} %join.2.refs_0_), channel_id=1, source_target_pairs={{0,2},{1,3},{2,0},{3,1},{4,6},{5,7},{6,4},{7,5},{8,10},{9,11},{10,... | collective-permute-start | bytes 479240 | tf_op jit(solution)/shard_map/ppermute | solution.py:671
  24.7 2.8 %collective-permute-done.7.refs_3_ = bf16[48,1664]{1,0:T(8,128)(2,1)S(1)} collective-permute-done((bf16[48,1664]{1,0:T(8,128)(2,1)S(1)}, bf16[48,1664]{1,0:T(8,128)(2,1)S(1)}, u32[]{:S(2)}, u32[]{:S(2)}) %collective-permute-start.7) | collective-permute-done | bytes 159776 | tf_op jit(solution)/shard_map/ppermute | solution.py:671
  27.5 1.4 collective-permute-done.6.refs_2_
  29.5 1.1 collective-permute-start.11
  30.6 1.4 prepare.1
  32.1 7.5 %forward.1 = (bf16[640,768]{1,0:T(8,128)(2,1)S(1)}, bf16[160,768]{1,0:T(8,128)(2,1)S(1)}, bf16[160,768]{1,0:T(8,128)(2,1)S(1)}, bf16[160,768]{1,0:T(8,128)(2,1)S...) custom-call(f32[1024,384]{1,0:T(8,128)S(1)} %get-tuple-element.149.x, ...), custom_call_target="tpu_custom_call" | custom-call | bytes 1024 | tf_op jit(solution)/shard_map/forward/pallas_call | solution.py:41
  42.4 0.7 collective-permute-start.17
  43.1 0.8 collective-permute-start.18
  43.9 5.8 %collective-permute-done.10.whole = bf16[768,384]{1,0:T(8,128)(2,1)S(1)} collective-permute-done((bf16[768,384]{1,0:T(8,128)(2,1)S(1)}, bf16[768,384]{1,0:T(8,128)(2,1)S(1)}, u32[]{:S(2)}, u32[]{:S(2)}) %collective-permute-start.10) | collective-permute-done | bytes 589856 | tf_op jit(solution)/shard_map/ppermute | solution.py:671
  49.7 1.1 collective-permute-start.16
  50.8 1.0 collective-permute-start.20
  51.8 1.0 collective-permute-start.19
  52.9 6.8 %collective-permute-done.16.refs_3_ = bf16[384,384]{1,0:T(8,128)(2,1)S(1)} collective-permute-done((bf16[384,384]{1,0:T(8,128)(2,1)S(1)}, bf16[384,384]{1,0:T(8,128)(2,1)S(1)}, u32[]{:S(2)}, u32[]{:S(2)}) %collective-permute-start.16) | collective-permute-done | bytes 294944 | tf_op jit(solution)/shard_map/ppermute | solution.py:671
  60.2 5.8 %collective-permute-done.20.refs_2_ = bf16[384,384]{1,0:T(8,128)(2,1)S(1)} collective-permute-done((bf16[384,384]{1,0:T(8,128)(2,1)S(1)}, bf16[384,384]{1,0:T(8,128)(2,1)S(1)}, u32[]{:S(2)}, u32[]{:S(2)}) %collective-permute-start.20) | collective-permute-done | bytes 294944 | tf_op jit(solution)/shard_map/ppermute | solution.py:671
  66.0 5.3 %collective-permute-done.19.near_out = bf16[384,384]{1,0:T(8,128)(2,1)S(1)} collective-permute-done((bf16[384,384]{1,0:T(8,128)(2,1)S(1)}, bf16[384,384]{1,0:T(8,128)(2,1)S(1)}, u32[]{:S(2)}, u32[]{:S(2)}) %collective-permute-start.19) | collective-permute-done | bytes 294944 | tf_op jit(solution)/shard_map/ppermute | solution.py:671
  74.6 5.6 %expert.3 = (bf16[320,768]{1,0:T(8,128)(2,1)S(1)}, bf16[320,768]{1,0:T(8,128)(2,1)S(1)}, bf16[640,1536]{1,0:T(8,128)(2,1)S(1)}, bf16[640,1536]{1,0:T(8,128)(2,1)S(1)}) custom-call(bf16[320,768]{1,0:T(8,128)(2,1)S(1)} %collective-permute-done.18.refs_0_.refs_2_, bf16[320,768]{1,0:T(8,128)(2,1)S(1)} %collective-permute-done.25.refs_1_.refs_3_, ...), custom_call_target="tpu_custom_call" | custom-call | flops 3019898880 | bytes 1024 | tf_op jit(solution)/shard_map/expert/pallas_call | solution.py:41
  80.2 5.5 %expert.2 = (bf16[320,768]{1,0:T(8,128)(2,1)S(1)}, bf16[320,768]{1,0:T(8,128)(2,1)S(1)}, bf16[640,1536]{1,0:T(8,128)(2,1)S(1)}, bf16[640,1536]{1,0:T(8,128)(2,1)S(1)}) custom-call(bf16[320,768]{1,0:T(8,128)(2,1)S(1)} %get-tuple-element.180.refs_0_, bf16[320,768]{1,0:T(8,128)(2,1)S(1)} %collective-permute-done.17.refs_1_, ...), custom_call_target="tpu_custom_call" | custom-call | flops 3019898880 | bytes 1024 | tf_op jit(solution)/shard_map/expert/pallas_call | solution.py:41
  85.7 4.0 %expert_grad.1 = (bf16[1536,384]{1,0:T(8,128)(2,1)S(1)}, bf16[1536,384]{1,0:T(8,128)(2,1)S(1)}) custom-call(bf16[320,768]{1,0:T(8,128)(2,1)S(1)} %get-tuple-element.180.refs_0_, bf16[320,768]{1,0:T(8,128)(2,1)S(1)} %collective-permute-done.17.refs_1_, bf16[320,768]{1,0:T(8,128)(2,1)S(1)} %collective-permute-done.18.refs_0_.refs_2_, ...), custom_call_target="tpu_custom_call" | custom-call | flops 3019898880 | bytes 1024 | tf_op jit(solution)/shard_map/expert_grad/pallas_call | solution.py:41
  90.4 3.0 %collective-permute-start.28 = (bf16[320,768]{1,0:T(8,128)(2,1)S(1)}, bf16[320,768]{1,0:T(8,128)(2,1)S(1)}, u32[]{:S(2)}, u32[]{:S(2)}) collective-permute-start(bf16[320,768]{1,0:T(8,128)(2,1)S(1)} %get-tuple-element.210), channel_id=1, source_target_pairs={{0,8},{1,9},{2,10},{3,11},{4,12},{5,13},{6,14},{7,15},{8,0},{9,1},... | collective-permute-start | bytes 1474568 | tf_op jit(solution)/shard_map/ppermute | solution.py:671
  93.4 1.0 split.1
  94.5 0.7 collective-permute-start.30
  95.1 1.4 collective-permute-start.31
  96.6 17.4 %collective-permute-done.27.refs_1_ = bf16[320,768]{1,0:T(8,128)(2,1)S(1)} collective-permute-done((bf16[320,768]{1,0:T(8,128)(2,1)S(1)}, bf16[320,768]{1,0:T(8,128)(2,1)S(1)}, u32[]{:S(2)}, u32[]{:S(2)}) %collective-permute-start.27) | collective-permute-done | bytes 491552 | tf_op jit(solution)/shard_map/ppermute | solution.py:671
  114.1 1.1 collective-permute-done.28.refs_2_
  117.0 1.4 collective-permute-start.41
  118.4 5.1 %combine.1 = (bf16[512,384]{1,0:T(8,128)(2,1)}, f32[512,384]{1,0:T(8,128)S(1)}, bf16[512,384]{1,0:T(8,128)(2,1)S(1)}, bf16[384,512]{1,0:T(8,128)(2,1)S(1)}) custom-call(f32[512,384]{1,0:T(8,128)S(1)} %get-tuple-element.163.middle, bf16[512,384]{1,0:T(8,128)(2,1)S(1)} %get-tuple-element.164.normed_two, f32[512,128]{1,0:T(8,128)S(1)} %get-tuple-element.165.probs, ...), custom_call_target="tpu_custom_call" | custom-call | flops 1509949440 | bytes 1024 | tf_op jit(solution)/shard_map/combine/pallas_call | solution.py:41
  123.6 9.5 %backward.1 = (bf16[512,384]{1,0:T(8,128)(2,1)S(1)}, bf16[208,768]{1,0:T(8,128)(2,1)S(1)}, bf16[208,768]{1,0:T(8,128)(2,1)S(1)}, f32[512,768]{1,0:T(8,128)S(1)},...) custom-call(bf16[1024,1152]{1,0:T(8,128)(2,1)S(1)} %get-tuple-elemen, ...), custom_call_target="tpu_custom_call" | custom-call | bytes 1024 | tf_op jit(solution)/shard_map/backward/pallas_call | solution.py:41
  136.4 2.5 %collective-permute-start.44 = (bf16[48,1664]{1,0:T(8,128)(2,1)S(1)}, bf16[48,1664]{1,0:T(8,128)(2,1)S(1)}, u32[]{:S(2)}, u32[]{:S(2)}) collective-permute-start(bf16[48,1664]{1,0:T(8,128)(2,1)S(1)} %get-tuple-element.242), channel_id=1, source_target_pairs={{0,6},{1,7},{2,4},{3,5},{4,2},{5,3},{6,0},{7,1},{8,14},{9,15},{10,... | collective-permute-start | bytes 479240 | tf_op jit(solution)/shard_map/ppermute | solution.py:671
  139.0 3.4 %collective-permute-done.42.refs_0_ = bf16[48,1664]{1,0:T(8,128)(2,1)S(1)} collective-permute-done((bf16[48,1664]{1,0:T(8,128)(2,1)S(1)}, bf16[48,1664]{1,0:T(8,128)(2,1)S(1)}, u32[]{:S(2)}, u32[]{:S(2)}) %collective-permute-start.42) | collective-permute-done | bytes 159776 | tf_op jit(solution)/shard_map/ppermute | solution.py:671
  142.4 3.1 %collective-permute-done.43.refs_1_ = bf16[48,1664]{1,0:T(8,128)(2,1)S(1)} collective-permute-done((bf16[48,1664]{1,0:T(8,128)(2,1)S(1)}, bf16[48,1664]{1,0:T(8,128)(2,1)S(1)}, u32[]{:S(2)}, u32[]{:S(2)}) %collective-permute-start.43) | collective-permute-done | bytes 159776 | tf_op jit(solution)/shard_map/ppermute | solution.py:671
  145.7 1.9 %collective-permute-start.47 = (bf16[208,768]{1,0:T(8,128)(2,1)S(1)}, bf16[208,768]{1,0:T(8,128)(2,1)S(1)}, u32[]{:S(2)}, u32[]{:S(2)}) collective-permute-start(bf16[208,768]{1,0:T(8,128)(2,1)S(1)} %get-tuple-element.252), channel_id=1, source_target_pairs={{0,1},{1,2},{2,3},{3,4},{4,5},{5,6},{6,7},{7,8},{8,9},{9,10},{10,1... | collective-permute-start | bytes 958472 | tf_op jit(solution)/shard_map/ppermute | solution.py:958
  147.6 1.3 collective-permute-start.48
  149.0 5.3 %collective-permute-start.46 = (bf16[12,1664]{1,0:T(8,128)(2,1)S(1)}, bf16[12,1664]{1,0:T(8,128)(2,1)S(1)}, u32[]{:S(2)}, u32[]{:S(2)}) collective-permute-start(bf16[12,1664]{1,0:T(8,128)(2,1)S(1)} %get-tuple-element.249), channel_id=1, source_target_pairs={{0,8},{1,9},{2,10},{3,11},{4,12},{5,13},{6,14},{7,15},{8,0},{9,1},... | collective-permute-start | bytes 119816 | tf_op jit(solution)/shard_map/ppermute | solution.py:671
  154.3 1.7 %collective-permute-start.49 = (bf16[12,1664]{1,0:T(8,128)(2,1)S(1)}, bf16[12,1664]{1,0:T(8,128)(2,1)S(1)}, u32[]{:S(2)}, u32[]{:S(2)}) collective-permute-start(bf16[12,1664]{1,0:T(8,128)(2,1)S(1)} %get-tuple-element.260), channel_id=1, source_target_pairs={{0,16},{1,17},{2,18},{3,19},{4,20},{5,21},{6,22},{7,23},{8,24},{9,... | collective-permute-start | bytes 119816 | tf_op jit(solution)/shard_map/ppermute | solution.py:671
  156.0 1.4 collective-permute-start.50
  157.5 2.4 %finish.1 = bf16[512,384]{1,0:T(8,128)(2,1)} custom-call(bf16[512,384]{1,0:T(8,128)(2,1)S(1)} %get-tuple-element.250.dq, f32[512,768]{1,0:T(8,128)S(1)} %get-tuple-element.251.inner, bf16[208,768]{1,0:T(8,128)(2,1)S(1)} %collective-permute-done.47.from_low, bf16[208,768]{1,0:T(8,128)(2,1)S(1)} %collective-permute-done.48.from_high, ...), custom_call_target="tpu_custom_call" | custom-call | flops 754974720 | bytes 1024 | tf_op jit(solution)/shard_map/finish/pallas_call | solution.py:41
  160.2 3.5 %collective-permute-done.49.refs_1_ = bf16[12,1664]{1,0:T(8,128)(2,1)S(1)} collective-permute-done((bf16[12,1664]{1,0:T(8,128)(2,1)S(1)}, bf16[12,1664]{1,0:T(8,128)(2,1)S(1)}, u32[]{:S(2)}, u32[]{:S(2)}) %collective-permute-start.49) | collective-permute-done | bytes 39968 | tf_op jit(solution)/shard_map/ppermute | solution.py:671
  163.8 1.3 final.1
  (91 shorter events, 14.5 us)
Async XLA Ops:
  2.1 15.4 %collective-permute-start.1 = (bf16[208,512]{1,0:T(8,128)(2,1)S(1)}, bf16[208,512]{1,0:T(8,128)(2,1)S(1)}, u32[]{:S(2)}, u32[]{:S(2)}) collective-permute-start(bf16[208,512]{1,0:T(8,128)(2,1)S(1)} %get-tuple-element.144), channel_id=1, source_target_pairs={{0,1},{1,2},{2,3},{3,4},{4,5},{5,6},{6,7},{7,8},{8,9},{9,10},{10,1... | collective-permute-start | bytes 638984 | tf_op jit(solution)/shard_map/ppermute | solution.py:743
  4.5 13.0 %collective-permute-start.2 = (bf16[208,512]{1,0:T(8,128)(2,1)S(1)}, bf16[208,512]{1,0:T(8,128)(2,1)S(1)}, u32[]{:S(2)}, u32[]{:S(2)}) collective-permute-start(bf16[208,512]{1,0:T(8,128)(2,1)S(1)} %get-tuple-element.145), channel_id=1, source_target_pairs={{1,0},{2,1},{3,2},{4,3},{5,4},{6,5},{7,6},{8,7},{9,8},{10,9},{11,1... | collective-permute-start | bytes 638984 | tf_op jit(solution)/shard_map/ppermute | solution.py:744
  5.8 11.7 %collective-permute-start = (bf16[12,1664]{1,0:T(8,128)(2,1)S(1)}, bf16[12,1664]{1,0:T(8,128)(2,1)S(1)}, u32[]{:S(2)}, u32[]{:S(2)}) collective-permute-start(bf16[12,1664]{1,0:T(8,128)(2,1)S(1)} %get-tuple-element.143.refs_0_), channel_id=1, source_target_pairs={{0,8},{1,9},{2,10},{3,11},{4,12},{5,13},{6,14},{7,15},{8,0},{9,1},... | collective-permute-start | bytes 119816 | tf_op jit(solution)/shard_map/ppermute | solution.py:671
  12.6 6.4 %collective-permute-start.3 = (bf16[12,1664]{1,0:T(8,128)(2,1)S(1)}, bf16[12,1664]{1,0:T(8,128)(2,1)S(1)}, u32[]{:S(2)}, u32[]{:S(2)}) collective-permute-start(bf16[12,1664]{1,0:T(8,128)(2,1)S(1)} %get-tuple-element.143.refs_0_), channel_id=1, source_target_pairs={{0,16},{1,17},{2,18},{3,19},{4,20},{5,21},{6,22},{7,23},{8,24},{9,... | collective-permute-start | bytes 119816 | tf_op jit(solution)/shard_map/ppermute | solution.py:671
  15.2 5.9 %collective-permute-start.4 = (bf16[12,1664]{1,0:T(8,128)(2,1)S(1)}, bf16[12,1664]{1,0:T(8,128)(2,1)S(1)}, u32[]{:S(2)}, u32[]{:S(2)}) collective-permute-start(bf16[12,1664]{1,0:T(8,128)(2,1)S(1)} %get-tuple-element.143.refs_0_), channel_id=1, source_target_pairs={{0,24},{1,25},{2,26},{3,27},{4,28},{5,29},{6,30},{7,31},{8,16},{9,... | collective-permute-start | bytes 119816 | tf_op jit(solution)/shard_map/ppermute | solution.py:671
  21.2 6.3 %collective-permute-start.7 = (bf16[48,1664]{1,0:T(8,128)(2,1)S(1)}, bf16[48,1664]{1,0:T(8,128)(2,1)S(1)}, u32[]{:S(2)}, u32[]{:S(2)}) collective-permute-start(bf16[48,1664]{1,0:T(8,128)(2,1)S(1)} %join.2.refs_0_), channel_id=1, source_target_pairs={{0,6},{1,7},{2,4},{3,5},{4,2},{5,3},{6,0},{7,1},{8,14},{9,15},{10,... | collective-permute-start | bytes 479240 | tf_op jit(solution)/shard_map/ppermute | solution.py:671
  21.9 7.0 %collective-permute-start.6 = (bf16[48,1664]{1,0:T(8,128)(2,1)S(1)}, bf16[48,1664]{1,0:T(8,128)(2,1)S(1)}, u32[]{:S(2)}, u32[]{:S(2)}) collective-permute-start(bf16[48,1664]{1,0:T(8,128)(2,1)S(1)} %join.2.refs_0_), channel_id=1, source_target_pairs={{0,4},{1,5},{2,6},{3,7},{4,0},{5,1},{6,2},{7,3},{8,12},{9,13},{10,... | collective-permute-start | bytes 479240 | tf_op jit(solution)/shard_map/ppermute | solution.py:671
  22.4 6.5 %collective-permute-start.5 = (bf16[48,1664]{1,0:T(8,128)(2,1)S(1)}, bf16[48,1664]{1,0:T(8,128)(2,1)S(1)}, u32[]{:S(2)}, u32[]{:S(2)}) collective-permute-start(bf16[48,1664]{1,0:T(8,128)(2,1)S(1)} %join.2.refs_0_), channel_id=1, source_target_pairs={{0,2},{1,3},{2,0},{3,1},{4,6},{5,7},{6,4},{7,5},{8,10},{9,11},{10,... | collective-permute-start | bytes 479240 | tf_op jit(solution)/shard_map/ppermute | solution.py:671
  24.7 25.0 %collective-permute-start.10 = (bf16[768,384]{1,0:T(8,128)(2,1)S(1)}, bf16[768,384]{1,0:T(8,128)(2,1)S(1)}, u32[]{:S(2)}, u32[]{:S(2)}) collective-permute-start(bf16[768,384]{1,0:T(8,128)(2,1)S(1)} %quarter.1.near_one), channel_id=1, source_target_pairs={{0,16},{1,17},{2,18},{3,19},{4,20},{5,21},{6,22},{7,23},{8,24},{9,... | collective-permute-start | bytes 1769480 | tf_op jit(solution)/shard_map/ppermute | solution.py:671
  28.9 3.1 %collective-permute-start.8 = (bf16[96,1664]{1,0:T(8,128)(2,1)S(1)}, bf16[96,1664]{1,0:T(8,128)(2,1)S(1)}, u32[]{:S(2)}, u32[]{:S(2)}) collective-permute-start(bf16[96,1664]{1,0:T(8,128)(2,1)S(1)} %get-tuple-element.161.near_one), channel_id=1, source_target_pairs={{0,1},{1,0},{2,3},{3,2},{4,5},{5,4},{6,7},{7,6},{8,9},{9,8},{10,11... | collective-permute-start | bytes 958472 | tf_op jit(solution)/shard_map/ppermute | solution.py:671
  29.0 3.0 %collective-permute-start.9 = (bf16[96,1664]{1,0:T(8,128)(2,1)S(1)}, bf16[96,1664]{1,0:T(8,128)(2,1)S(1)}, u32[]{:S(2)}, u32[]{:S(2)}) collective-permute-start(bf16[96,1664]{1,0:T(8,128)(2,1)S(1)} %get-tuple-element.162.near_two), channel_id=1, source_target_pairs={{0,1},{1,0},{2,3},{3,2},{4,5},{5,4},{6,7},{7,6},{8,9},{9,8},{10,11... | collective-permute-start | bytes 958472 | tf_op jit(solution)/shard_map/ppermute | solution.py:671
  29.5 10.1 %collective-permute-start.11 = (bf16[384,384]{1,0:T(8,128)(2,1)S(1)}, bf16[384,384]{1,0:T(8,128)(2,1)S(1)}, u32[]{:S(2)}, u32[]{:S(2)}) collective-permute-start(bf16[384,384]{1,0:T(8,128)(2,1)S(1)} %bitcast.15), channel_id=1, source_target_pairs={{0,2},{1,3},{2,0},{3,1},{4,6},{5,7},{6,4},{7,5},{8,10},{9,11},{10,... | collective-permute-start | bytes 884744 | tf_op jit(solution)/shard_map/ppermute | solution.py:671
  39.6 1.6 collective-permute-start.12
  39.7 1.9 %collective-permute-start.13 = (bf16[160,768]{1,0:T(8,128)(2,1)S(1)}, bf16[160,768]{1,0:T(8,128)(2,1)S(1)}, u32[]{:S(2)}, u32[]{:S(2)}) collective-permute-start(bf16[160,768]{1,0:T(8,128)(2,1)S(1)} %get-tuple-element.176), channel_id=1, source_target_pairs={{0,1},{1,0},{2,3},{3,2},{4,5},{5,4},{6,7},{7,6},{8,9},{9,8},{10,11... | collective-permute-start | bytes 737288 | tf_op jit(solution)/shard_map/ppermute | solution.py:671
  40.2 1.7 %collective-permute-start.14 = (bf16[160,768]{1,0:T(8,128)(2,1)S(1)}, bf16[160,768]{1,0:T(8,128)(2,1)S(1)}, u32[]{:S(2)}, u32[]{:S(2)}) collective-permute-start(bf16[160,768]{1,0:T(8,128)(2,1)S(1)} %get-tuple-element.177), channel_id=1, source_target_pairs={{0,1},{1,0},{2,3},{3,2},{4,5},{5,4},{6,7},{7,6},{8,9},{9,8},{10,11... | collective-permute-start | bytes 737288 | tf_op jit(solution)/shard_map/ppermute | solution.py:671
  40.3 2.0 %collective-permute-start.15 = (bf16[160,768]{1,0:T(8,128)(2,1)S(1)}, bf16[160,768]{1,0:T(8,128)(2,1)S(1)}, u32[]{:S(2)}, u32[]{:S(2)}) collective-permute-start(bf16[160,768]{1,0:T(8,128)(2,1)S(1)} %get-tuple-element.178), channel_id=1, source_target_pairs={{0,1},{1,0},{2,3},{3,2},{4,5},{5,4},{6,7},{7,6},{8,9},{9,8},{10,11... | collective-permute-start | bytes 737288 | tf_op jit(solution)/shard_map/ppermute | solution.py:671
  42.4 17.3 %collective-permute-start.17 = (bf16[320,768]{1,0:T(8,128)(2,1)S(1)}, bf16[320,768]{1,0:T(8,128)(2,1)S(1)}, u32[]{:S(2)}, u32[]{:S(2)}) collective-permute-start(bf16[320,768]{1,0:T(8,128)(2,1)S(1)} %get-tuple-element.183), channel_id=1, source_target_pairs={{0,4},{1,5},{2,6},{3,7},{4,0},{5,1},{6,2},{7,3},{8,12},{9,13},{10,... | collective-permute-start | bytes 1474568 | tf_op jit(solution)/shard_map/ppermute | solution.py:671
  43.1 17.2 %collective-permute-start.18 = (bf16[320,768]{1,0:T(8,128)(2,1)S(1)}, bf16[320,768]{1,0:T(8,128)(2,1)S(1)}, u32[]{:S(2)}, u32[]{:S(2)}) collective-permute-start(bf16[320,768]{1,0:T(8,128)(2,1)S(1)} %get-tuple-element.184), channel_id=1, source_target_pairs={{0,8},{1,9},{2,10},{3,11},{4,12},{5,13},{6,14},{7,15},{8,0},{9,1},... | collective-permute-start | bytes 1474568 | tf_op jit(solution)/shard_map/ppermute | solution.py:671
  49.7 9.9 %collective-permute-start.16 = (bf16[384,384]{1,0:T(8,128)(2,1)S(1)}, bf16[384,384]{1,0:T(8,128)(2,1)S(1)}, u32[]{:S(2)}, u32[]{:S(2)}) collective-permute-start(bf16[384,384]{1,0:T(8,128)(2,1)S(1)} %get-tuple-element.182.refs_1_), channel_id=1, source_target_pairs={{0,2},{1,3},{2,0},{3,1},{4,6},{5,7},{6,4},{7,5},{8,10},{9,11},{10,... | collective-permute-start | bytes 884744 | tf_op jit(solution)/shard_map/ppermute | solution.py:671
  50.8 15.2 %collective-permute-start.20 = (bf16[384,384]{1,0:T(8,128)(2,1)S(1)}, bf16[384,384]{1,0:T(8,128)(2,1)S(1)}, u32[]{:S(2)}, u32[]{:S(2)}) collective-permute-start(bf16[384,384]{1,0:T(8,128)(2,1)S(1)} %get-tuple-element.188.refs_0_), channel_id=1, source_target_pairs={{0,2},{1,3},{2,0},{3,1},{4,6},{5,7},{6,4},{7,5},{8,10},{9,11},{10,... | collective-permute-start | bytes 884744 | tf_op jit(solution)/shard_map/ppermute | solution.py:671
  51.8 19.4 %collective-permute-start.19 = (bf16[384,384]{1,0:T(8,128)(2,1)S(1)}, bf16[384,384]{1,0:T(8,128)(2,1)S(1)}, u32[]{:S(2)}, u32[]{:S(2)}) collective-permute-start(bf16[384,384]{1,0:T(8,128)(2,1)S(1)} %bitcast.16), channel_id=1, source_target_pairs={{0,2},{1,3},{2,0},{3,1},{4,6},{5,7},{6,4},{7,5},{8,10},{9,11},{10,... | collective-permute-start | bytes 884744 | tf_op jit(solution)/shard_map/ppermute | solution.py:671
  59.7 13.1 %collective-permute-start.25 = (bf16[320,768]{1,0:T(8,128)(2,1)S(1)}, bf16[320,768]{1,0:T(8,128)(2,1)S(1)}, u32[]{:S(2)}, u32[]{:S(2)}) collective-permute-start(bf16[320,768]{1,0:T(8,128)(2,1)S(1)} %get-tuple-element.197), channel_id=1, source_target_pairs={{0,12},{1,13},{2,14},{3,15},{4,8},{5,9},{6,10},{7,11},{8,4},{9,5},... | collective-permute-start | bytes 1474568 | tf_op jit(solution)/shard_map/ppermute | solution.py:671
  71.7 1.6 collective-permute-start.21
  71.7 2.0 %collective-permute-start.22 = (bf16[384,384]{1,0:T(8,128)(2,1)S(1)}, bf16[384,384]{1,0:T(8,128)(2,1)S(1)}, u32[]{:S(2)}, u32[]{:S(2)}) collective-permute-start(bf16[384,384]{1,0:T(8,128)(2,1)S(1)} %get-tuple-element.192), channel_id=1, source_target_pairs={{0,1},{1,0},{2,3},{3,2},{4,5},{5,4},{6,7},{7,6},{8,9},{9,8},{10,11... | collective-permute-start | bytes 884744 | tf_op jit(solution)/shard_map/ppermute | solution.py:671
  72.2 1.9 %collective-permute-start.23 = (bf16[384,384]{1,0:T(8,128)(2,1)S(1)}, bf16[384,384]{1,0:T(8,128)(2,1)S(1)}, u32[]{:S(2)}, u32[]{:S(2)}) collective-permute-start(bf16[384,384]{1,0:T(8,128)(2,1)S(1)} %get-tuple-element.193), channel_id=1, source_target_pairs={{0,1},{1,0},{2,3},{3,2},{4,5},{5,4},{6,7},{7,6},{8,9},{9,8},{10,11... | collective-permute-start | bytes 884744 | tf_op jit(solution)/shard_map/ppermute | solution.py:671
  72.3 2.3 %collective-permute-start.24 = (bf16[384,384]{1,0:T(8,128)(2,1)S(1)}, bf16[384,384]{1,0:T(8,128)(2,1)S(1)}, u32[]{:S(2)}, u32[]{:S(2)}) collective-permute-start(bf16[384,384]{1,0:T(8,128)(2,1)S(1)} %get-tuple-element.194), channel_id=1, source_target_pairs={{0,1},{1,0},{2,3},{3,2},{4,5},{5,4},{6,7},{7,6},{8,9},{9,8},{10,11... | collective-permute-start | bytes 884744 | tf_op jit(solution)/shard_map/ppermute | solution.py:671
  89.7 3.7 %collective-permute-start.26 = (bf16[1536,384]{1,0:T(8,128)(2,1)S(1)}, bf16[1536,384]{1,0:T(8,128)(2,1)S(1)}, u32[]{:S(2)}, u32[]{:S(2)}) collective-permute-start(bf16[1536,384]{1,0:T(8,128)(2,1)S(1)} %get-tuple-element.203), channel_id=1, source_target_pairs={{0,1},{1,0},{2,3},{3,2},{4,5},{5,4},{6,7},{7,6},{8,9},{9,8},{10,11... | collective-permute-start | bytes 3538952 | tf_op jit(solution)/shard_map/ppermute | solution.py:671
  89.9 24.0 %collective-permute-start.27 = (bf16[320,768]{1,0:T(8,128)(2,1)S(1)}, bf16[320,768]{1,0:T(8,128)(2,1)S(1)}, u32[]{:S(2)}, u32[]{:S(2)}) collective-permute-start(bf16[320,768]{1,0:T(8,128)(2,1)S(1)} %get-tuple-element.208), channel_id=1, source_target_pairs={{0,4},{1,5},{2,6},{3,7},{4,0},{5,1},{6,2},{7,3},{8,12},{9,13},{10,... | collective-permute-start | bytes 1474568 | tf_op jit(solution)/shard_map/ppermute | solution.py:671
  90.4 23.7 %collective-permute-start.29 = (bf16[320,768]{1,0:T(8,128)(2,1)S(1)}, bf16[320,768]{1,0:T(8,128)(2,1)S(1)}, u32[]{:S(2)}, u32[]{:S(2)}) collective-permute-start(bf16[320,768]{1,0:T(8,128)(2,1)S(1)} %get-tuple-element.211), channel_id=1, source_target_pairs={{0,12},{1,13},{2,14},{3,15},{4,8},{5,9},{6,10},{7,11},{8,4},{9,5},... | collective-permute-start | bytes 1474568 | tf_op jit(solution)/shard_map/ppermute | solution.py:671
  90.4 24.8 %collective-permute-start.28 = (bf16[320,768]{1,0:T(8,128)(2,1)S(1)}, bf16[320,768]{1,0:T(8,128)(2,1)S(1)}, u32[]{:S(2)}, u32[]{:S(2)}) collective-permute-start(bf16[320,768]{1,0:T(8,128)(2,1)S(1)} %get-tuple-element.210), channel_id=1, source_target_pairs={{0,8},{1,9},{2,10},{3,11},{4,12},{5,13},{6,14},{7,15},{8,0},{9,1},... | collective-permute-start | bytes 1474568 | tf_op jit(solution)/shard_map/ppermute | solution.py:671
  94.5 19.5 %collective-permute-start.30 = (bf16[384,384]{1,0:T(8,128)(2,1)S(1)}, bf16[384,384]{1,0:T(8,128)(2,1)S(1)}, u32[]{:S(2)}, u32[]{:S(2)}) collective-permute-start(bf16[384,384]{1,0:T(8,128)(2,1)S(1)} %get-tuple-element.213), channel_id=1, source_target_pairs={{0,2},{1,3},{2,0},{3,1},{4,6},{5,7},{6,4},{7,5},{8,10},{9,11},{10,... | collective-permute-start | bytes 884744 | tf_op jit(solution)/shard_map/ppermute | solution.py:671
  95.1 18.8 %collective-permute-start.31 = (bf16[384,384]{1,0:T(8,128)(2,1)S(1)}, bf16[384,384]{1,0:T(8,128)(2,1)S(1)}, u32[]{:S(2)}, u32[]{:S(2)}) collective-permute-start(bf16[384,384]{1,0:T(8,128)(2,1)S(1)} %get-tuple-element.214), channel_id=1, source_target_pairs={{0,2},{1,3},{2,0},{3,1},{4,6},{5,7},{6,4},{7,5},{8,10},{9,11},{10,... | collective-permute-start | bytes 884744 | tf_op jit(solution)/shard_map/ppermute | solution.py:671
  115.3 1.7 %collective-permute-start.32 = (bf16[160,768]{1,0:T(8,128)(2,1)S(1)}, bf16[160,768]{1,0:T(8,128)(2,1)S(1)}, u32[]{:S(2)}, u32[]{:S(2)}) collective-permute-start(bf16[160,768]{1,0:T(8,128)(2,1)S(1)} %get-tuple-element.217), channel_id=1, source_target_pairs={{0,1},{1,0},{2,3},{3,2},{4,5},{5,4},{6,7},{7,6},{8,9},{9,8},{10,11... | collective-permute-start | bytes 737288 | tf_op jit(solution)/shard_map/ppermute | solution.py:671
  115.4 3.0 %collective-permute-start.33 = (bf16[160,768]{1,0:T(8,128)(2,1)S(1)}, bf16[160,768]{1,0:T(8,128)(2,1)S(1)}, u32[]{:S(2)}, u32[]{:S(2)}) collective-permute-start(bf16[160,768]{1,0:T(8,128)(2,1)S(1)} %get-tuple-element.218), channel_id=1, source_target_pairs={{0,1},{1,0},{2,3},{3,2},{4,5},{5,4},{6,7},{7,6},{8,9},{9,8},{10,11... | collective-permute-start | bytes 737288 | tf_op jit(solution)/shard_map/ppermute | solution.py:671
  115.9 2.6 %collective-permute-start.34 = (bf16[160,768]{1,0:T(8,128)(2,1)S(1)}, bf16[160,768]{1,0:T(8,128)(2,1)S(1)}, u32[]{:S(2)}, u32[]{:S(2)}) collective-permute-start(bf16[160,768]{1,0:T(8,128)(2,1)S(1)} %get-tuple-element.219), channel_id=1, source_target_pairs={{0,1},{1,0},{2,3},{3,2},{4,5},{5,4},{6,7},{7,6},{8,9},{9,8},{10,11... | collective-permute-start | bytes 737288 | tf_op jit(solution)/shard_map/ppermute | solution.py:671
  116.0 2.5 %collective-permute-start.35 = (bf16[160,768]{1,0:T(8,128)(2,1)S(1)}, bf16[160,768]{1,0:T(8,128)(2,1)S(1)}, u32[]{:S(2)}, u32[]{:S(2)}) collective-permute-start(bf16[160,768]{1,0:T(8,128)(2,1)S(1)} %get-tuple-element.220), channel_id=1, source_target_pairs={{0,1},{1,0},{2,3},{3,2},{4,5},{5,4},{6,7},{7,6},{8,9},{9,8},{10,11... | collective-permute-start | bytes 737288 | tf_op jit(solution)/shard_map/ppermute | solution.py:671
  116.4 17.3 %collective-permute-start.40 = (bf16[384,384]{1,0:T(8,128)(2,1)S(1)}, bf16[384,384]{1,0:T(8,128)(2,1)S(1)}, u32[]{:S(2)}, u32[]{:S(2)}) collective-permute-start(bf16[384,384]{1,0:T(8,128)(2,1)S(1)} %get-tuple-element.233), channel_id=1, source_target_pairs={{0,2},{1,3},{2,0},{3,1},{4,6},{5,7},{6,4},{7,5},{8,10},{9,11},{10,... | collective-permute-start | bytes 884744 | tf_op jit(solution)/shard_map/ppermute | solution.py:671
  117.0 16.7 %collective-permute-start.41 = (bf16[384,384]{1,0:T(8,128)(2,1)S(1)}, bf16[384,384]{1,0:T(8,128)(2,1)S(1)}, u32[]{:S(2)}, u32[]{:S(2)}) collective-permute-start(bf16[384,384]{1,0:T(8,128)(2,1)S(1)} %get-tuple-element.234), channel_id=1, source_target_pairs={{0,2},{1,3},{2,0},{3,1},{4,6},{5,7},{6,4},{7,5},{8,10},{9,11},{10,... | collective-permute-start | bytes 884744 | tf_op jit(solution)/shard_map/ppermute | solution.py:671
  118.4 27.3 %collective-permute-start.45 = (bf16[768,384]{1,0:T(8,128)(2,1)S(1)}, bf16[768,384]{1,0:T(8,128)(2,1)S(1)}, u32[]{:S(2)}, u32[]{:S(2)}) collective-permute-start(bf16[768,384]{1,0:T(8,128)(2,1)S(1)} %away.1), channel_id=1, source_target_pairs={{0,16},{1,17},{2,18},{3,19},{4,20},{5,21},{6,22},{7,23},{8,24},{9,... | collective-permute-start | bytes 1769480 | tf_op jit(solution)/shard_map/ppermute | solution.py:671
  133.1 1.6 collective-permute-start.37
  135.4 7.0 %collective-permute-start.42 = (bf16[48,1664]{1,0:T(8,128)(2,1)S(1)}, bf16[48,1664]{1,0:T(8,128)(2,1)S(1)}, u32[]{:S(2)}, u32[]{:S(2)}) collective-permute-start(bf16[48,1664]{1,0:T(8,128)(2,1)S(1)} %get-tuple-element.240), channel_id=1, source_target_pairs={{0,2},{1,3},{2,0},{3,1},{4,6},{5,7},{6,4},{7,5},{8,10},{9,11},{10,... | collective-permute-start | bytes 479240 | tf_op jit(solution)/shard_map/ppermute | solution.py:671
  136.1 9.4 %collective-permute-start.43 = (bf16[48,1664]{1,0:T(8,128)(2,1)S(1)}, bf16[48,1664]{1,0:T(8,128)(2,1)S(1)}, u32[]{:S(2)}, u32[]{:S(2)}) collective-permute-start(bf16[48,1664]{1,0:T(8,128)(2,1)S(1)} %get-tuple-element.241), channel_id=1, source_target_pairs={{0,4},{1,5},{2,6},{3,7},{4,0},{5,1},{6,2},{7,3},{8,12},{9,13},{10,... | collective-permute-start | bytes 479240 | tf_op jit(solution)/shard_map/ppermute | solution.py:671
  136.4 9.1 %collective-permute-start.44 = (bf16[48,1664]{1,0:T(8,128)(2,1)S(1)}, bf16[48,1664]{1,0:T(8,128)(2,1)S(1)}, u32[]{:S(2)}, u32[]{:S(2)}) collective-permute-start(bf16[48,1664]{1,0:T(8,128)(2,1)S(1)} %get-tuple-element.242), channel_id=1, source_target_pairs={{0,6},{1,7},{2,4},{3,5},{4,2},{5,3},{6,0},{7,1},{8,14},{9,15},{10,... | collective-permute-start | bytes 479240 | tf_op jit(solution)/shard_map/ppermute | solution.py:671
  145.7 11.7 %collective-permute-start.47 = (bf16[208,768]{1,0:T(8,128)(2,1)S(1)}, bf16[208,768]{1,0:T(8,128)(2,1)S(1)}, u32[]{:S(2)}, u32[]{:S(2)}) collective-permute-start(bf16[208,768]{1,0:T(8,128)(2,1)S(1)} %get-tuple-element.252), channel_id=1, source_target_pairs={{0,1},{1,2},{2,3},{3,4},{4,5},{5,6},{6,7},{7,8},{8,9},{9,10},{10,1... | collective-permute-start | bytes 958472 | tf_op jit(solution)/shard_map/ppermute | solution.py:958
  147.6 9.8 %collective-permute-start.48 = (bf16[208,768]{1,0:T(8,128)(2,1)S(1)}, bf16[208,768]{1,0:T(8,128)(2,1)S(1)}, u32[]{:S(2)}, u32[]{:S(2)}) collective-permute-start(bf16[208,768]{1,0:T(8,128)(2,1)S(1)} %get-tuple-element.253), channel_id=1, source_target_pairs={{1,0},{2,1},{3,2},{4,3},{5,4},{6,5},{7,6},{8,7},{9,8},{10,9},{11,1... | collective-permute-start | bytes 958472 | tf_op jit(solution)/shard_map/ppermute | solution.py:957
  149.0 11.2 %collective-permute-start.46 = (bf16[12,1664]{1,0:T(8,128)(2,1)S(1)}, bf16[12,1664]{1,0:T(8,128)(2,1)S(1)}, u32[]{:S(2)}, u32[]{:S(2)}) collective-permute-start(bf16[12,1664]{1,0:T(8,128)(2,1)S(1)} %get-tuple-element.249), channel_id=1, source_target_pairs={{0,8},{1,9},{2,10},{3,11},{4,12},{5,13},{6,14},{7,15},{8,0},{9,1},... | collective-permute-start | bytes 119816 | tf_op jit(solution)/shard_map/ppermute | solution.py:671
  154.3 9.4 %collective-permute-start.49 = (bf16[12,1664]{1,0:T(8,128)(2,1)S(1)}, bf16[12,1664]{1,0:T(8,128)(2,1)S(1)}, u32[]{:S(2)}, u32[]{:S(2)}) collective-permute-start(bf16[12,1664]{1,0:T(8,128)(2,1)S(1)} %get-tuple-element.260), channel_id=1, source_target_pairs={{0,16},{1,17},{2,18},{3,19},{4,20},{5,21},{6,22},{7,23},{8,24},{9,... | collective-permute-start | bytes 119816 | tf_op jit(solution)/shard_map/ppermute | solution.py:671
  156.0 7.7 %collective-permute-start.50 = (bf16[12,1664]{1,0:T(8,128)(2,1)S(1)}, bf16[12,1664]{1,0:T(8,128)(2,1)S(1)}, u32[]{:S(2)}, u32[]{:S(2)}) collective-permute-start(bf16[12,1664]{1,0:T(8,128)(2,1)S(1)} %get-tuple-element.261), channel_id=1, source_target_pairs={{0,24},{1,25},{2,26},{3,27},{4,28},{5,29},{6,30},{7,31},{8,16},{9,... | collective-permute-start | bytes 119816 | tf_op jit(solution)/shard_map/ppermute | solution.py:671
  (11 other events, 174.2 us)
